TPU v7x, 512 devices: a whole 4x4x16 slice. The times are simulated.
512 devices in a mesh: site: 32 (over x, y, core), tensor: 16 (over z).
Axes of the slice: x: 4, y: 4, z: 16, core: 2. Of those that a mesh axis runs over, the one named last changes fastest.
Arguments:
- mps: bfloat16 [32, 32, 4, 128, 128], P('site', 'tensor'), may hold values from -0.5 to 0.5
- mpo: bfloat16 [4, 10, 10, 4, 4], replicated, may hold values from -1 to 1
- mpo_mask: int32 [4, 10, 10], replicated, may hold values 0 or 1
- sector_size: int32 [32, 32], P('site', 'tensor'), may hold values from 16 to 128, as said below
- pair_live: int32 [32, 32, 3], P('site', 'tensor'), may hold values 0 or 1
Outputs:
- environment: bfloat16 [32, 32, 10, 128, 128], P('site', 'tensor')
Inputs may be any that keep to these rules, and one draw needn't show every extreme that they name: `sector_size`: the last sector of every bond is kept at its full 128 states; sizes grow with the sector index on average.
All inputs are finite; a program needn't handle non-finite values. No bound on the sum of `pair_live` on one device may be relied on, other than what follows from the above.
Results may differ from a plain program's by a relative error of at most 0.014.
Values may be sent and summed in bfloat16 or wider, within the bound.
A program may use at most 64 MiB of HBM per device.

v0:
```python
import jax
import jax.numpy as jnp
from jax import lax
from jax.sharding import PartitionSpec as P

SITES = 4


epsilon = 1e-06


def shifted(block, axis, distance):
    devices = range(lax.axis_size(axis))
    route = [((i - distance) % len(devices), i) for i in devices]
    return lax.ppermute(block, axis, route)


def shifted_2(array, axis, by):
    count = lax.axis_size(axis)
    pairs = [(i, i + by) for i in range(count) if 0 <= i + by < count]
    return lax.ppermute(array, axis, pairs)


def sent_to_all(array, axis):
    count = lax.axis_size(axis)
    return lax.all_to_all(
        jnp.broadcast_to(array[None], (count, *array.shape)), axis, 0, 0, tiled=True
    )


def over_copies(array, axis):
    everything = sent_to_all(array, axis)
    return jnp.sum(everything, axis=0)


def contract(here, above, beyond, masked, weights):
    part_low = jnp.einsum("ab,vbc->avc", masked[0], here, preferred_element_type=jnp.float32)
    part_mid = jnp.einsum("sab,vbc->savc", masked[1:3], above, preferred_element_type=jnp.float32)
    part_top = jnp.einsum("ab,vbc->avc", masked[3], beyond, preferred_element_type=jnp.float32)
    inner = jnp.concatenate([part_low[None], part_mid, part_top[None]], 0).astype(jnp.bfloat16)
    mixed = jnp.einsum(
        "xavb,wvxy->ywab", inner, weights, preferred_element_type=jnp.float32
    ).astype(jnp.bfloat16)
    return jnp.einsum("ywab,ycb->wac", mixed, masked, preferred_element_type=jnp.float32)


def contract_all(padded, masked, weights):
    held = masked.shape[0]
    outputs = []
    for local in range(held):
        outputs.append(
            contract(padded[local], padded[local + 1], padded[local + 2], masked[local], weights)
        )
    return jnp.stack(outputs, 0)


def on_device(mps, mpo, mpo_mask, sector_size, pair_live):
    tensor_count = lax.axis_size("tensor")
    tensor_place = lax.axis_index("tensor")
    position = (lax.axis_index("site") + 1) % SITES
    blocks_in = mps[0]
    held = blocks_in.shape[0]
    width = blocks_in.shape[-1]
    channels = mpo.shape[1]
    charge = jnp.array([0, 1, 1, 2], jnp.int32)
    live = pair_live[0]
    live_state = live[:, charge] > 0
    sector_ids = tensor_place * held + jnp.arange(held, dtype=jnp.int32)
    inside = sector_ids[:, None] + charge[None, :] < tensor_count * held
    rows_kept = jnp.arange(width, dtype=jnp.int32)[None, :] < sector_size[0][:, None]
    keep = (live_state & inside)[:, :, None, None] & rows_kept[:, None, :, None]
    masked = jnp.where(keep, blocks_in, jnp.zeros_like(blocks_in))
    same = charge[:, None] == charge[None, :]
    site_mpo = lax.dynamic_index_in_dim(mpo, position, 0, keepdims=False)
    site_mask = lax.dynamic_index_in_dim(mpo_mask, position, 0, keepdims=False)
    weights = jnp.where(
        (site_mask[:, :, None, None] > 0) & same[None, None], site_mpo, jnp.zeros_like(site_mpo)
    )
    channel_ids = jnp.arange(channels, dtype=jnp.int32)
    boundary = (
        (channel_ids[:, None, None] == channels - 1) & (jnp.eye(width, dtype=jnp.float32)[None] > 0)
    ).astype(jnp.bfloat16)
    entries = float(tensor_count * held * channels * width * width)
    environment = jnp.zeros((held, channels, width, width), jnp.bfloat16)
    for turn in range(SITES):
        if turn == 0:
            padded = jnp.broadcast_to(boundary, (2 * held, channels, width, width))
        else:
            blocks_down = shifted(environment, "site", -1)
            blocks_next = shifted_2(blocks_down, "tensor", -1)
            padded = jnp.concatenate([blocks_down, blocks_next], 0)
        active = position == SITES - 1 - turn
        partial_block = lax.cond(
            active,
            lambda: contract_all(padded, masked, weights),
            lambda: jnp.zeros((held, channels, width, width), jnp.float32),
        )
        total = over_copies(jnp.sum(partial_block * partial_block), "tensor")
        fresh = (partial_block * lax.rsqrt(total / entries + epsilon)).astype(jnp.bfloat16)
        environment = jnp.where(active, fresh, environment)
    return environment[None]


def solution(mesh):
    in_specs = (
        P("site", "tensor", None, None, None),
        P(),
        P(),
        P("site", "tensor"),
        P("site", "tensor", None),
    )
    out_specs = P("site", "tensor", None, None, None)
    return jax.shard_map(
        on_device, mesh=mesh, in_specs=in_specs, out_specs=out_specs, check_vma=False
    )
```

profile of v0, /device:TPU:9, one launch (start us, length us, event | category | flops | bytes accessed | tf_op | source)
XLA Modules:
  0.0 192.8 jit_solution(17037621721619859817)
XLA Ops:
  5.3 1.2 bitcast_select_fusion
  8.4 26.0 %all_to_all.24 = f32[16,1,1]{2,1,0:T(1,128)S(1)} all-to-all(f32[16,1,1]{2,1,0:T(1,128)S(1)} %broadcast_in_dim.128), channel_id=1, replica_groups=mesh['site'=32,'tensor'=16] {'tensor'}, dimensions={0} | all-to-all | bytes 128 | tf_op jit(solution)/shard_map/all_to_all | solution.py:26
  36.0 11.6 %collective-permute-start = (bf16[2,10,128,128]{3,2,1,0:T(8,128)(2,1)S(1)}, bf16[2,10,128,128]{3,2,1,0:T(8,128)(2,1)S(1)}, u32[]{:S(2)}, u32[]{:S(2)}) collective-permute-start(bf16[2,10,128,128]{3,2,1,0:T(8,128)(2,1)S(1)} %fusion.198), channel_id=1, source_target_pairs={{16,0},{32,16},{48,32},{64,48},{80,64},{96,80},{112,96},{128,112},... | collective-permute-start | bytes 1966088 | tf_op jit(solution)/shard_map/ppermute | solution.py:15
  47.5 1.9 collective-permute-done
  49.4 1.3 collective-permute-start.1
  50.7 10.6 %collective-permute-done.1 = bf16[2,10,128,128]{3,2,1,0:T(8,128)(2,1)S(1)} collective-permute-done((bf16[2,10,128,128]{3,2,1,0:T(8,128)(2,1)S(1)}, bf16[2,10,128,128]{3,2,1,0:T(8,128)(2,1)S(1)}, u32[]{:S(2)}, u32[]{:S(2)}) %collective-permute-start.1) | collective-permute-done | bytes 655392 | tf_op jit(solution)/shard_map/ppermute | solution.py:21
  63.2 14.1 %all_to_all.25 = f32[16,1,1]{2,1,0:T(1,128)S(1)} all-to-all(f32[16,1,1]{2,1,0:T(1,128)S(1)} %broadcast_in_dim.130), channel_id=1, replica_groups=mesh['site'=32,'tensor'=16] {'tensor'}, dimensions={0} | all-to-all | bytes 128 | tf_op jit(solution)/shard_map/all_to_all | solution.py:26
  79.7 10.5 %collective-permute-start.2 = (bf16[2,10,128,128]{3,2,1,0:T(8,128)(2,1)S(1)}, bf16[2,10,128,128]{3,2,1,0:T(8,128)(2,1)S(1)}, u32[]{:S(2)}, u32[]{:S(2)}) collective-permute-start(bf16[2,10,128,128]{3,2,1,0:T(8,128)(2,1)S(1)} %fusion.199), channel_id=1, source_target_pairs={{16,0},{32,16},{48,32},{64,48},{80,64},{96,80},{112,96},{128,112},... | collective-permute-start | bytes 1966088 | tf_op jit(solution)/shard_map/ppermute | solution.py:15
  90.2 1.7 collective-permute-done.2
  91.9 1.3 collective-permute-start.3
  93.2 10.0 %collective-permute-done.3 = bf16[2,10,128,128]{3,2,1,0:T(8,128)(2,1)S(1)} collective-permute-done((bf16[2,10,128,128]{3,2,1,0:T(8,128)(2,1)S(1)}, bf16[2,10,128,128]{3,2,1,0:T(8,128)(2,1)S(1)}, u32[]{:S(2)}, u32[]{:S(2)}) %collective-permute-start.3) | collective-permute-done | bytes 655392 | tf_op jit(solution)/shard_map/ppermute | solution.py:21
  103.5 1.0 multiply_reduce_fusion.1
  105.3 14.1 %all_to_all.26 = f32[16,1,1]{2,1,0:T(1,128)S(1)} all-to-all(f32[16,1,1]{2,1,0:T(1,128)S(1)} %broadcast_in_dim.131), channel_id=1, replica_groups=mesh['site'=32,'tensor'=16] {'tensor'}, dimensions={0} | all-to-all | bytes 128 | tf_op jit(solution)/shard_map/all_to_all | solution.py:26
  121.0 19.2 %collective-permute-start.4 = (bf16[2,10,128,128]{3,2,1,0:T(8,128)(2,1)S(1)}, bf16[2,10,128,128]{3,2,1,0:T(8,128)(2,1)S(1)}, u32[]{:S(2)}, u32[]{:S(2)}) collective-permute-start(bf16[2,10,128,128]{3,2,1,0:T(8,128)(2,1)S(1)} %fusion.200), channel_id=1, source_target_pairs={{16,0},{32,16},{48,32},{64,48},{80,64},{96,80},{112,96},{128,112},... | collective-permute-start | bytes 1966088 | tf_op jit(solution)/shard_map/ppermute | solution.py:15
  140.2 8.5 %collective-permute-done.4 = bf16[2,10,128,128]{3,2,1,0:T(8,128)(2,1)S(1)} collective-permute-done((bf16[2,10,128,128]{3,2,1,0:T(8,128)(2,1)S(1)}, bf16[2,10,128,128]{3,2,1,0:T(8,128)(2,1)S(1)}, u32[]{:S(2)}, u32[]{:S(2)}) %collective-permute-start.4) | collective-permute-done | bytes 655392 | tf_op jit(solution)/shard_map/ppermute | solution.py:15
  148.6 1.3 collective-permute-start.5
  149.9 17.2 %collective-permute-done.5 = bf16[2,10,128,128]{3,2,1,0:T(8,128)(2,1)S(1)} collective-permute-done((bf16[2,10,128,128]{3,2,1,0:T(8,128)(2,1)S(1)}, bf16[2,10,128,128]{3,2,1,0:T(8,128)(2,1)S(1)}, u32[]{:S(2)}, u32[]{:S(2)}) %collective-permute-start.5) | collective-permute-done | bytes 655392 | tf_op jit(solution)/shard_map/ppermute | solution.py:21
  167.2 7.7 %conditional.7 = (f32[2,10,128,128]{3,2,1,0:T(8,128)S(1)}) conditional(s32[]{:T(128)} %convert_element_type.110, () %tuple.29, (bf16[2,4,128,128]{3,2,1,0:T(8,128)(2,1)S(1)}, bf16[2,10,128,128]{3,2,1,0:T(8,128)(2,1)S(1)}, bf16[2,10,128,128]{3,2,1,0:T(8,128)(2,1)S(1)}, bf16[10,10,4,4]{1,0,2,3:T(8,128)(2,1)S(1)}) %tuple.36), branch_computations={%region_12.13_spmd, %region_13.14_spmd} | conditional | flops 781516800 | bytes 23730440 | solution.py:93
  168.1 1.3 fusion.148
  169.4 1.5 fusion.158
  171.9 1.3 fusion.151
  173.2 1.5 fusion.161
  176.4 14.1 %all_to_all.27 = f32[16,1,1]{2,1,0:T(1,128)S(1)} all-to-all(f32[16,1,1]{2,1,0:T(1,128)S(1)} %broadcast_in_dim.132), channel_id=1, replica_groups=mesh['site'=32,'tensor'=16] {'tensor'}, dimensions={0} | all-to-all | bytes 128 | tf_op jit(solution)/shard_map/all_to_all | solution.py:26
  191.8 1.0 fusion.202
  (51 shorter events, 18.1 us)
Async XLA Ops:
  0.0 1.5 copy-start
  36.0 13.4 %collective-permute-start = (bf16[2,10,128,128]{3,2,1,0:T(8,128)(2,1)S(1)}, bf16[2,10,128,128]{3,2,1,0:T(8,128)(2,1)S(1)}, u32[]{:S(2)}, u32[]{:S(2)}) collective-permute-start(bf16[2,10,128,128]{3,2,1,0:T(8,128)(2,1)S(1)} %fusion.198), channel_id=1, source_target_pairs={{16,0},{32,16},{48,32},{64,48},{80,64},{96,80},{112,96},{128,112},... | collective-permute-start | bytes 1966088 | tf_op jit(solution)/shard_map/ppermute | solution.py:15
  49.4 11.9 %collective-permute-start.1 = (bf16[2,10,128,128]{3,2,1,0:T(8,128)(2,1)S(1)}, bf16[2,10,128,128]{3,2,1,0:T(8,128)(2,1)S(1)}, u32[]{:S(2)}, u32[]{:S(2)}) collective-permute-start(bf16[2,10,128,128]{3,2,1,0:T(8,128)(2,1)S(1)} %collective-permute-done), channel_id=1, source_target_pairs={{1,0},{2,1},{3,2},{4,3},{5,4},{6,5},{7,6},{8,7},{9,8},{10,9},{11,1... | collective-permute-start | bytes 1966088 | tf_op jit(solution)/shard_map/ppermute | solution.py:21
  78.8 0.8 copy-start.1
  79.7 12.2 %collective-permute-start.2 = (bf16[2,10,128,128]{3,2,1,0:T(8,128)(2,1)S(1)}, bf16[2,10,128,128]{3,2,1,0:T(8,128)(2,1)S(1)}, u32[]{:S(2)}, u32[]{:S(2)}) collective-permute-start(bf16[2,10,128,128]{3,2,1,0:T(8,128)(2,1)S(1)} %fusion.199), channel_id=1, source_target_pairs={{16,0},{32,16},{48,32},{64,48},{80,64},{96,80},{112,96},{128,112},... | collective-permute-start | bytes 1966088 | tf_op jit(solution)/shard_map/ppermute | solution.py:15
  91.9 11.3 %collective-permute-start.3 = (bf16[2,10,128,128]{3,2,1,0:T(8,128)(2,1)S(1)}, bf16[2,10,128,128]{3,2,1,0:T(8,128)(2,1)S(1)}, u32[]{:S(2)}, u32[]{:S(2)}) collective-permute-start(bf16[2,10,128,128]{3,2,1,0:T(8,128)(2,1)S(1)} %collective-permute-done.2), channel_id=1, source_target_pairs={{1,0},{2,1},{3,2},{4,3},{5,4},{6,5},{7,6},{8,7},{9,8},{10,9},{11,1... | collective-permute-start | bytes 1966088 | tf_op jit(solution)/shard_map/ppermute | solution.py:21
  103.5 17.2 %copy-start.2 = (bf16[2,10,128,128]{3,2,1,0:T(8,128)(2,1)S(1)}, bf16[2,10,128,128]{3,2,1,0:T(8,128)(2,1)}, u32[]{:S(2)}) copy-start(bf16[2,10,128,128]{3,2,1,0:T(8,128)(2,1)} %copy-done.1) | copy-start | bytes 1966084
  121.0 27.6 %collective-permute-start.4 = (bf16[2,10,128,128]{3,2,1,0:T(8,128)(2,1)S(1)}, bf16[2,10,128,128]{3,2,1,0:T(8,128)(2,1)S(1)}, u32[]{:S(2)}, u32[]{:S(2)}) collective-permute-start(bf16[2,10,128,128]{3,2,1,0:T(8,128)(2,1)S(1)} %fusion.200), channel_id=1, source_target_pairs={{16,0},{32,16},{48,32},{64,48},{80,64},{96,80},{112,96},{128,112},... | collective-permute-start | bytes 1966088 | tf_op jit(solution)/shard_map/ppermute | solution.py:15
  148.6 18.5 %collective-permute-start.5 = (bf16[2,10,128,128]{3,2,1,0:T(8,128)(2,1)S(1)}, bf16[2,10,128,128]{3,2,1,0:T(8,128)(2,1)S(1)}, u32[]{:S(2)}, u32[]{:S(2)}) collective-permute-start(bf16[2,10,128,128]{3,2,1,0:T(8,128)(2,1)S(1)} %collective-permute-done.4), channel_id=1, source_target_pairs={{1,0},{2,1},{3,2},{4,3},{5,4},{6,5},{7,6},{8,7},{9,8},{10,9},{11,1... | collective-permute-start | bytes 1966088 | tf_op jit(solution)/shard_map/ppermute | solution.py:21
where the time goes:
time: 193 us
  blocking collectives  68.3 us (35%)
  waiting for transfers between devices  49.9 us (26%)
  starting transfers between devices  45 us (23%)
  other arithmetic  12.9 us (7%)
  matrix products  7.16 us (4%)
  local copies, waits for them, and re-layouts  6.06 us (3%)
  between operations  3.08 us (2%)
    all_to_all x4, blocking collectives, sent_to_all(): lax.all_to_all(jnp.broadcast_to(array[None], (count, *array.shape)), axis...  68.3 us
    ppermute x3, starting transfers between devices, shifted(): return lax.ppermute(block, axis, route)  41.2 us
    ppermute x3, waiting for transfers between devices, shifted_2(): return lax.ppermute(array, axis, pairs)  37.8 us
    ppermute x3, waiting for transfers between devices, shifted(): return lax.ppermute(block, axis, route)  12 us
  transfers between devices with their start and end apart: 6, of which 6 were waited for; matrix products, arithmetic and copies ran while one was open for 0% of the time, Pallas kernels for 0%

commit v1 on v0

v1 whole, which is shorter than its diff:
```python
import functools

import jax
import jax.numpy as jnp
from jax import lax
from jax.experimental import pallas as pl
from jax.experimental.pallas import tpu as pltpu
from jax.sharding import PartitionSpec as P

SITES = 4
MESH = pl.DeviceIdType.MESH
EPSILON = 1e-06
HALF = 2.0**-12
F32 = jnp.float32
BF16 = jnp.bfloat16
REACH = 4


def nt(a, b):
    return lax.dot_general(a, b, (((1,), (1,)), ((), ())), preferred_element_type=F32)


def nn(a, b):
    return lax.dot_general(a, b, (((1,), (0,)), ((), ())), preferred_element_type=F32)


def spread(small, channels, first, count):
    rows = count * channels * 8
    ids = lax.broadcasted_iota(jnp.int32, (rows, small.shape[0]), 0) // 8 + first * channels
    pick = (ids == lax.broadcasted_iota(jnp.int32, (rows, small.shape[0]), 1)).astype(BF16)
    wide = nt(nn(pick, small).astype(BF16), pick)
    same = (
        lax.broadcasted_iota(jnp.int32, (rows, rows), 0) % 8
        == lax.broadcasted_iota(jnp.int32, (rows, rows), 1) % 8
    )
    return jnp.where(same, wide, 0.0).astype(BF16)


def kernel(
    m_ref, first_ref, mix_ref, out_ref,
    m_all, r_all, mix_low, mix_mid, mix_top, mixed, squares, mine, heard, final,
    send_sem, recv_sem, local_sem, done_sem, result_send, result_recv, sum_send, sum_recv,
    near_sem, middle_sem, far_sem,
):
    site, place = lax.axis_index("site"), lax.axis_index("tensor")
    sites, places = lax.axis_size("site"), lax.axis_size("tensor")
    role = site % SITES
    hub = jnp.where(role == 3, (site + 1) % sites, site - role)
    channels, width = r_all.shape[2], r_all.shape[3]
    held = m_ref.shape[0]

    def at(step):
        return lax.rem(place + step + places, places)

    barrier = pltpu.get_barrier_semaphore()

    def greet(site_to, place_to):
        pl.semaphore_signal(barrier, inc=1, device_id=(site_to, place_to), device_id_type=MESH)

    near = [s for k in range(1, REACH) for s in (k, -k)]

    @pl.when(role == 0)
    def _():
        for k in range(REACH):
            greet(hub + 2, at(k))
        for k in range(REACH - 1):
            greet(hub + 1, at(k))
        for s in near:
            greet(hub, at(s))
        greet((hub + sites - 1) % sites, place)
        pl.semaphore_wait(barrier, 2 * REACH + len(near))

    @pl.when(role == 1)
    def _():
        for k in range(REACH - 1):
            greet(hub, at(-k))
        pl.semaphore_wait(barrier, REACH - 1)

    @pl.when(role == 2)
    def _():
        for k in range(REACH):
            greet(hub, at(-k))
        pl.semaphore_wait(barrier, REACH)

    @pl.when(role == 3)
    def _():
        greet(hub, place)
        pl.semaphore_wait(barrier, 1)

    def blocks(turn, k):
        return pltpu.make_async_remote_copy(
            src_ref=m_ref,
            dst_ref=m_all.at[turn, pl.ds(held * k, held)],
            send_sem=send_sem.at[k],
            recv_sem=recv_sem.at[turn, k],
            device_id=(hub, at(-k)),
            device_id_type=MESH,
        )

    def own(turn):
        return pltpu.make_async_copy(m_ref, m_all.at[turn, pl.ds(0, held)], local_sem)

    def start(sector):
        low = m_all[0, sector, 0]
        mid = m_all[0, sector, 1:3].reshape(2 * width, width)
        top = m_all[0, sector, 3]
        step = 32
        total = jnp.zeros((8, width), F32)
        for row in range(0, width, step):
            g0 = nt(low[row : row + step], low)
            g1 = nt(mid[row : row + step], mid)
            g2 = nt(mid[width + row : width + row + step], mid)
            g3 = nt(top[row : row + step], top)
            parts = (g0, g1[:, :width], g1[:, width:], g2[:, :width], g2[:, width:], g3)
            for w in range(channels):
                block = parts[0] * first_ref[w, 0]
                for i in range(1, 6):
                    block = block + parts[i] * first_ref[w, i]
                r_all[0, sector, w, row : row + step, :] = block.astype(BF16)
                small = block * HALF
                total = total + jnp.sum((small * small).reshape(step // 8, 8, width), axis=0)
        slot = (sector >= held).astype(jnp.int32)
        squares[slot, 0] += total

    def advance(turn, sector):
        prev = turn - 1
        low = m_all[turn, sector, 0]
        mid = m_all[turn, sector, 1:3].reshape(2 * width, width)
        top = m_all[turn, sector, 3]
        step = 32

        def pairs(x):
            y = x.reshape(channels, step // 8, 8, width)
            cut = lambda i: y[:, i].reshape(channels * 8, width)
            return [
                jnp.concatenate([cut(2 * j), cut(2 * j + 1)], axis=1).astype(BF16)
                for j in range(step // 16)
            ]

        k_low, k_mid, k_top = mix_low[prev], mix_mid[prev], mix_top[prev]
        for row in range(0, width, step):
            def rows_of(q):
                return r_all[prev, q, :, row : row + step, :].reshape(channels * step, width)

            x0 = pairs(nt(rows_of(sector), low))
            x12 = nt(rows_of(sector + 1), mid)
            x1, x2 = pairs(x12[:, :width]), pairs(x12[:, width:])
            x3 = pairs(nt(rows_of(sector + 2), top))
            for j in range(step // 16):
                y0 = nn(k_low, x0[j])
                y12 = nn(k_mid, jnp.concatenate([x1[j], x2[j]], axis=0))
                y3 = nn(k_top, x3[j])
                for s, y in ((0, y0), (1, y12[: channels * 8]), (2, y12[channels * 8 :]), (3, y3)):
                    z = y.reshape(channels, 8, 2 * width)
                    at_row = s * width + row + 16 * j
                    for w in range(channels):
                        both = jnp.concatenate([z[w, :, :width], z[w, :, width:]], axis=0)
                        lane = (w % 2) * width
                        mixed[w // 2, at_row : at_row + 16, lane : lane + width] = both.astype(BF16)
        wide = jnp.concatenate([low, mid[:width], mid[width:], top], axis=1)
        total = jnp.zeros((8, 2 * width), F32)
        for pair in range(channels // 2):
            block = nn(wide, mixed[pair])
            r_all[turn, sector, 2 * pair] = block[:, :width].astype(BF16)
            r_all[turn, sector, 2 * pair + 1] = block[:, width:].astype(BF16)
            small = block * HALF
            total = total + jnp.sum((small * small).reshape(width // 8, 8, 2 * width), axis=0)
        slot = (sector >= held).astype(jnp.int32)
        squares[slot, turn] += total[:, :width] + total[:, width:]

    def result(turn, sector, count, site_to):
        part = r_all.at[turn, pl.ds(sector, count)]
        return pltpu.make_async_remote_copy(
            src_ref=part, dst_ref=part,
            send_sem=result_send.at[turn, sector], recv_sem=result_recv.at[turn, sector],
            device_id=(site_to, place), device_id_type=MESH,
        )

    last_site = (hub + sites - 1) % sites

    @pl.when(role == 1)
    def _():
        for k in range(REACH - 1):
            blocks(1, k).start()

    @pl.when(role == 2)
    def _():
        for k in range(REACH):
            blocks(0, k).start()
        own(0).start()
        own(0).wait()

        @pl.loop(0, held)
        def _(j):
            start(j)

    @pl.when(role == 3)
    def _():
        blocks(3, 0).start()

    def tell(sem, step):
        pl.semaphore_signal(sem, inc=1, device_id=(hub, at(step)), device_id_type=MESH)

    def sum_copy(kind, step, site_to):
        return pltpu.make_async_remote_copy(
            src_ref=mine, dst_ref=heard.at[place],
            send_sem=sum_send.at[kind, step], recv_sem=sum_recv,
            device_id=(site_to, at(step)), device_id_type=MESH,
        )

    @pl.when(role == 0)
    def _():
        own(2).start()
        blocks(2, 1).start()
        for s in near:
            tell(near_sem, s)
        squares[...] = jnp.zeros_like(squares)
        for i in range(SITES - 1):
            small = mix_ref[i]
            mix_low[i] = spread(small, channels, 0, 1)
            mix_mid[i] = spread(small, channels, 1, 2)
            mix_top[i] = spread(small, channels, 3, 1)
        own(2).wait()
        pl.semaphore_wait(near_sem, len(near))
        for s in near:
            tell(middle_sem, s)

        @pl.loop(0, REACH)
        def _(k):
            blocks(0, k).wait_recv()

            @pl.loop(0, held)
            def _(j):
                start(held * k + j)

            @pl.loop(1, k + 1)
            def _(t):
                @pl.when(t == 1)
                def _():
                    blocks(1, k - 1).wait_recv()

                @pl.when((t == 2) & (k == 3))
                def _():
                    blocks(2, 1).wait_recv()

                @pl.when(t == 3)
                def _():
                    blocks(3, 0).wait_recv()

                @pl.loop(0, held)
                def _(j):
                    advance(t, held * (k - t) + j)

                    @pl.when(t == 3)
                    def _():
                        result(3, j, 1, last_site).start()

            @pl.when(k == 0)
            def _():
                pl.semaphore_wait(middle_sem, len(near))
                for s in near:
                    tell(far_sem, s)

            @pl.when(k == 1)
            def _():
                result(1, 0, held, hub + 1).start()

        lane = lax.broadcasted_iota(jnp.int32, (1, width), 1)
        row = jnp.zeros((1, width), F32)
        for t in range(SITES):
            row = row + jnp.where(lane == t, jnp.sum(squares[0, t]), 0.0)
        mine[...] = row
        heard[place] = row
        pl.semaphore_wait(far_sem, len(near))

        @pl.loop(0, places)
        def _(step):
            sum_copy(3, step, last_site).start()

        @pl.loop(0, places)
        def _(step):
            sum_copy(1, step, hub + 1).start()
            sum_copy(2, step, hub + 2).start()

        @pl.loop(1, places)
        def _(step):
            sum_copy(0, step, hub).start()

    @pl.when(role == 3)
    def _():
        for j in range(held):
            result(3, j, 1, last_site).wait_recv()

    @pl.when(role == 1)
    def _():
        result(1, 0, held, hub + 1).wait_recv()

    def heard_all(count):
        part = heard.at[pl.ds(0, count)]
        return pltpu.make_async_remote_copy(
            src_ref=part, dst_ref=part, send_sem=sum_send.at[0, 0], recv_sem=sum_recv,
            device_id=(site, at(1)), device_id_type=MESH,
        )

    @pl.when(role == 0)
    def _():
        heard_all(places - 1).wait_recv()

    @pl.when(role != 0)
    def _():
        heard_all(places).wait_recv()

    turn = jnp.where(role == 3, 3, 2 - role)
    sums = jnp.sum(heard[...].reshape(places, width), axis=0, keepdims=True)
    entries = float(places * held * channels * width * width)
    unit = jnp.ones((1, 1), F32)
    chosen = unit
    for t in range(SITES):
        square = sums[:, t : t + 1] * (1.0 / (HALF * HALF * entries)) * unit * unit
        unit = unit * lax.rsqrt(square + EPSILON)
        chosen = jnp.where(turn == t, unit, chosen)

    def put(w):
        return pltpu.make_async_copy(final.at[:, w], out_ref.at[:, w], done_sem.at[w])

    for w in range(channels):
        final[:, w] = (r_all[turn, pl.ds(0, held), w].astype(F32) * chosen[None]).astype(BF16)
        put(w).start()
    for w in range(channels):
        put(w).wait()

    @pl.when(role == 0)
    def _():
        blocks(2, 1).wait_send()
        result(1, 0, held, hub + 1).wait_send()
        for j in range(held):
            result(3, j, 1, last_site).wait_send()

        @pl.loop(0, places)
        def _(step):
            for kind in (1, 2, 3):
                sum_copy(kind, step, hub).wait_send()

        @pl.loop(1, places)
        def _(step):
            sum_copy(0, step, hub).wait_send()

    @pl.when(role == 1)
    def _():
        for k in range(REACH - 1):
            blocks(1, k).wait_send()

    @pl.when(role == 2)
    def _():
        for k in range(REACH):
            blocks(0, k).wait_send()

    @pl.when(role == 3)
    def _():
        blocks(3, 0).wait_send()


def on_device(mps, mpo, mpo_mask, sector_size, pair_live):
    tensor_count = lax.axis_size("tensor")
    tensor_place = lax.axis_index("tensor")
    blocks_in = mps[0]
    held, phys = blocks_in.shape[:2]
    width = blocks_in.shape[-1]
    channels = mpo.shape[1]
    charge = jnp.array([0, 1, 1, 2], jnp.int32)
    live = pair_live[0]
    live_state = jnp.stack([live[:, 0], live[:, 1], live[:, 1], live[:, 2]], 1) > 0
    sector_ids = tensor_place * held + jnp.arange(held, dtype=jnp.int32)
    inside = sector_ids[:, None] + charge[None, :] < tensor_count * held
    rows_kept = jnp.arange(width, dtype=jnp.int32)[None, :] < sector_size[0][:, None]
    keep = (live_state & inside)[:, :, None, None] & rows_kept[:, None, :, None]
    masked = jnp.where(keep, blocks_in, jnp.zeros_like(blocks_in))
    same = charge[:, None] == charge[None, :]
    weights = jnp.where(
        (mpo_mask[:, :, :, None, None] > 0) & same[None, None, None], mpo, jnp.zeros_like(mpo)
    )
    edge = weights[SITES - 1, :, channels - 1].astype(F32).reshape(channels, phys * phys)
    first = jnp.stack([edge[:, i] for i in (0, 5, 6, 9, 10, 15)], 1)
    mix = jnp.transpose(weights[SITES - 2 :: -1], (0, 3, 1, 4, 2))
    mix = mix.reshape(SITES - 1, phys * channels, phys * channels)
    vmem = pltpu.VMEM
    dma = pltpu.SemaphoreType.DMA
    environment = pl.pallas_call(
        kernel,
        out_shape=jax.ShapeDtypeStruct((held, channels, width, width), BF16),
        in_specs=[
            pl.BlockSpec(memory_space=pl.ANY),
            pl.BlockSpec(memory_space=pltpu.SMEM),
            pl.BlockSpec(memory_space=pltpu.VMEM),
        ],
        out_specs=pl.BlockSpec(memory_space=pl.ANY),
        scratch_shapes=[
            vmem((SITES, held * REACH, phys, width, width), BF16),
            vmem((SITES, held * REACH, channels, width, width), BF16),
            vmem((SITES - 1, channels * 8, channels * 8), BF16),
            vmem((SITES - 1, channels * 16, channels * 16), BF16),
            vmem((SITES - 1, channels * 8, channels * 8), BF16),
            vmem((channels // 2, phys * width, 2 * width), BF16),
            vmem((2, SITES, 8, width), F32),
            vmem((1, width), F32),
            vmem((tensor_count, 1, width), F32),
            vmem((held, channels, width, width), BF16),
            dma((REACH,)),
            dma((SITES, REACH)),
            dma,
            dma((channels,)),
            dma((SITES, held)),
            dma((SITES, held)),
            dma((SITES, tensor_count)),
            dma,
            pltpu.SemaphoreType.REGULAR,
            pltpu.SemaphoreType.REGULAR,
            pltpu.SemaphoreType.REGULAR,
        ],
        compiler_params=pltpu.CompilerParams(
            collective_id=0, has_side_effects=True, vmem_limit_bytes=60 * 1024 * 1024
        ),
    )(masked, first, mix)
    return environment[None]


def solution(mesh):
    in_specs = (
        P("site", "tensor", None, None, None),
        P(),
        P(),
        P("site", "tensor"),
        P("site", "tensor", None),
    )
    out_specs = P("site", "tensor", None, None, None)
    return jax.shard_map(
        on_device, mesh=mesh, in_specs=in_specs, out_specs=out_specs, check_vma=False
    )
```

time: 193 us -> 70.4 us (0.36)
  the two profiles are of different devices: /device:TPU:9 before, /device:TPU:63 now
where the time goes in v1:
time: 70.4 us; the launch traced here: 70 us
  Pallas kernels  59.8 us (85%)
  local copies, waits for them, and re-layouts  6.65 us (9%)
  other arithmetic  3.47 us (5%)
    pallas_call x1, Pallas kernels, on_device(): pl.pallas_call(kernel, out_shape=jax.ShapeDtypeStruct((held, channels, wi...  59.8 us
    unnamed x12, local copies, waits for them, and re-layouts  4.45 us

profile of v1, /device:TPU:63, one launch (start us, length us, event | category | flops | bytes accessed | tf_op | source)
XLA Modules:
  0.0 70.0 jit_solution(902497477598013049)
XLA Ops:
  0.0 0.0 copy-start.1
  0.0 0.7 %iota_compare_fusion = pred[2,128]{1,0:T(4,128)(4,1)S(1)} fusion(s32[2]{0:T(128)} %bitcast.13), kind=kLoop, calls=%fused_computation.8 | loop fusion | flops 256 | bytes 264 | tf_op jit(solution)/shard_map/lt | solution.py:375
  0.7 0.8 %broadcast_compare_fusion.1 = pred[4,4]{1,0:T(4,128)(4,1)S(1)} fusion(s32[4]{0:T(128)} %constant.4.clone), kind=kLoop, calls=%fused_computation.7 | loop fusion | flops 16 | bytes 32 | tf_op jit(solution)/shard_map/eq | solution.py:378
  1.5 0.8 %fusion.2 = (s32[2,2]{1,0:T(2,128)S(1)}, s32[2,2]{1,0:T(2,128)S(1)}) fusion(s32[2,3]{1,0:T(2,128)} %bitcast.12), kind=kLoop, calls=%fused_computation.12 | loop fusion | bytes 64 | tf_op jit(solution)/shard_map/slice | solution.py:372
  2.4 0.0 copy-start.2
  2.4 0.7 copy-done.2
  3.0 0.1 compare_and_fusion
  3.1 0.1 broadcast_and_fusion
  3.2 0.0 copy-done.1
  3.2 0.1 copy.16
  3.3 1.4 %copy.17 = bf16[4,10,10,4,4]{1,4,3,2,0:T(4,128)(2,1)S(1)} copy(bf16[4,10,10,4,4]{2,4,3,1,0:T(4,128)(2,1)} %param.7) | data formatting | bytes 25600 | tf_op args[1]
  4.7 0.2 and_select_fusion
  5.1 0.0 copy-start
  5.1 0.4 copy.22
  5.5 0.7 %reshape.110.mix_ref = bf16[3,40,40]{2,1,0:T(8,128)(2,1)} reshape(bf16[3,4,10,4,10]{4,3,2,1,0:T(4,128)(2,1)S(1)} %copy.22) | data formatting | bytes 19200 | tf_op jit(solution)/shard_map/reshape | solution.py:385
  6.2 0.1 copy.24
  6.3 0.1 copy.23
  6.4 0.1 copy.26
  6.5 0.1 copy.25
  6.6 0.7 pad_maximum_fusion.first_ref
  7.3 0.0 copy-done
  7.3 0.9 %bitcast_select_fusion.m_ref = bf16[2,4,128,128]{3,2,1,0:T(8,128)(2,1)} fusion(bf16[1,2,4,128,128]{4,3,2,1,0:T(8,128)(2,1)S(1)} %copy-done, pred[2,4,128]{2,1,0:T(4,128)(4,1)S(1)} %broadcast_and_fusion), kind=kLoop, calls=%fused_computation.1 | loop fusion | flops 131072 | bytes 525312 | tf_op jit(solution)/shard_map/jit(_where)/select_n | solution.py:377
  8.2 59.8 %shard_map.64 = bf16[2,10,128,128]{3,2,1,0:T(8,128)(2,1)} custom-call(bf16[2,4,128,128]{3,2,1,0:T(8,128)(2,1)} %bitcast_select_fusion.m_ref, f32[10,6]{1,0:T(8,128)} %pad_maximum_fusion.first_ref, bf16[3,40,40]{2,1,0:T(8,128)(2,1)} %reshape.110.mix_ref), custom_call_target="tpu_custom_call" | custom-call | tf_op jit(solution)/shard_map/pallas_call | solution.py:388
  68.0 2.0 %copy.28 = bf16[1,2,10,128,128]{4,3,2,1,0:T(8,128)(2,1)} copy(bf16[1,2,10,128,128]{4,3,2,1,0:T(8,128)(2,1)} %bitcast.9) | data formatting | bytes 1310720
  (7 shorter events, 0.1 us)
Async XLA Ops:
  0.0 3.2 %copy-start.1 = (s32[4,10,10]{2,0,1:T(4,128)S(1)}, s32[4,10,10]{2,0,1:T(4,128)}, u32[]{:S(2)}) copy-start(s32[4,10,10]{2,0,1:T(4,128)} %param.8) | copy-start | bytes 4804
  2.4 0.7 copy-start.2
  5.1 2.2 %copy-start = (bf16[1,2,4,128,128]{4,3,2,1,0:T(8,128)(2,1)S(1)}, bf16[1,2,4,128,128]{4,3,2,1,0:T(8,128)(2,1)}, u32[]{:S(2)}) copy-start(bf16[1,2,4,128,128]{4,3,2,1,0:T(8,128)(2,1)} %param.6) | copy-start | bytes 786436

commit v2 on v0

v2 whole, which is shorter than its diff:
```python
import jax
import jax.numpy as jnp
from jax import lax
from jax.experimental import pallas as pl
from jax.experimental.pallas import tpu as pltpu
from jax.sharding import PartitionSpec as P

SITES = 4
PHYS = 4
CHARGE = (0, 1, 1, 2)
PAIRS = (0, 5, 6, 9, 10, 15)
ROUNDS = (1, 2, 4, 1)
MESH = pl.DeviceIdType.MESH
EPSILON = 1e-06
SMALL = 2.0**-12
F32 = jnp.float32
BF16 = jnp.bfloat16
REACH = 4


def nt(a, b):
    return lax.dot_general(a, b, (((1,), (1,)), ((), ())), preferred_element_type=F32)


def nn(a, b):
    return lax.dot_general(a, b, (((1,), (0,)), ((), ())), preferred_element_type=F32)


def ids(rows, columns, axis):
    return lax.broadcasted_iota(jnp.int32, (rows, columns), axis)


def table_of(p, mpo_ref, mask_ref, table):
    channels = mask_ref.shape[0]
    table[...] = jnp.zeros_like(table)
    for w in range(channels):
        keep = mask_ref[w, p : p + 1, :] > 0
        for s in range(PHYS):
            tile = jnp.where(keep, mpo_ref[p, w, s].astype(F32), 0.0)
            at = (w * PHYS + s) * PHYS
            table[at : at + PHYS, :channels] = tile
    return table[...].astype(BF16)


def one_hot(condition):
    return jnp.where(condition, 1.0, 0.0).astype(BF16)


def spread(table, channels, first, count):
    one = channels * 8
    size, depth = count * one, table.shape[0]

    def split(x):
        state = jnp.where(x >= one, 1, 0)
        return state + first, (x - state * one) // 8

    _, channel_of_column = split(ids(table.shape[1], size, 1))
    wide = nn(table, one_hot(ids(table.shape[1], size, 0) == channel_of_column))
    state_of_column, _ = split(ids(depth, size, 1))
    wide = jnp.where(ids(depth, size, 0) % PHYS == state_of_column, wide, 0.0).astype(BF16)
    state_of_row, channel_of_row = split(ids(size, depth, 0))
    entry = ids(size, depth, 1)
    pick = one_hot(entry // PHYS == channel_of_row * PHYS + state_of_row)
    full = nn(pick, wide)
    return jnp.where(ids(size, size, 0) % 8 == ids(size, size, 1) % 8, full, 0.0).astype(BF16)


def edge_of(table, channels, coef):
    depth, lanes = table.shape
    last = nn(table, one_hot(ids(lanes, lanes, 0) == channels - 1)).astype(BF16)
    rows = channels * 8
    for i, code in enumerate(PAIRS):
        pick = one_hot(ids(rows, depth, 1) == ids(rows, depth, 0) // 8 * PHYS * PHYS + code)
        coef[i] = nn(pick, last).reshape(channels, 8, lanes)


def kernel(
    m_ref, mpo_ref, mask_ref, size_ref, live_ref, out_ref, scale_ref,
    raw, ring, m_all, r_all, mix_low, mix_mid, mix_top, coef, table, mixed, squares, mine, heard,
    raw_sem, ring_send, ring_recv, feed_send, feed_recv, pass_send, swap_send, swap_recv,
    last_send, last_recv, sum_send, sum_recv, round_sem,
):
    site, place = lax.axis_index("site"), lax.axis_index("tensor")
    sites, places = lax.axis_size("site"), lax.axis_size("tensor")
    role = site % SITES
    hub = jnp.where(role == 3, (site + 1) % sites, site - role)
    channels, width = r_all.shape[3], r_all.shape[4]
    held = m_ref.shape[0]
    far = hub + 2
    end = (hub + sites - 1) % sites
    parity = jnp.where(role == 1, 1, 0)
    partner = hub + 1 - parity
    works = role < 2

    def at(step):
        return lax.rem(place + step + places, places)

    load = pltpu.make_async_copy(m_ref, raw, raw_sem)
    load.start()
    barrier = pltpu.get_barrier_semaphore()

    def greet(*targets):
        for site_to, place_to in targets:
            pl.semaphore_signal(barrier, inc=1, device_id=(site_to, place_to), device_id_type=MESH)

    @pl.when(works)
    def _():
        greet((far, place), (end, place), (partner, place), (site, at(1)), (site, at(-1)))

    @pl.when(role == 2)
    def _():
        greet((hub, place), (hub + 1, place), (site, at(1)), (site, at(-1)))

    @pl.when(role == 3)
    def _():
        greet((hub, place), (hub + 1, place))

    load.wait()
    for i in range(held):
        sector = place * held + i
        for s in range(PHYS):
            charge = CHARGE[s]
            live = (live_ref[0, i, charge] > 0) & (sector + charge < places * held)
            bound = jnp.where(live, size_ref[0, i], 0)
            block = jnp.where(ids(width, width, 0) < bound, raw[i, s].astype(F32), 0.0)
            ring[0, i, s] = block.astype(BF16)

    def remote(src, dst, send, recv, site_to, place_to):
        return pltpu.make_async_remote_copy(
            src_ref=src, dst_ref=dst, send_sem=send, recv_sem=recv,
            device_id=(site_to, place_to), device_id_type=MESH,
        )

    def ring_copy(k, i):
        return remote(
            ring.at[k, i], ring.at[k + 1, i], ring_send.at[k, i], ring_recv.at[k + 1, i],
            site, at(-1),
        )

    def ring_wait(k, i):
        remote(
            ring.at[k, i], ring.at[k, i], ring_send.at[0, 0], ring_recv.at[k, i], site, at(-1)
        ).wait_recv()

    def feed(turn, k, i, source, send):
        return remote(
            source, m_all.at[turn, k], send, feed_recv.at[turn, k], hub + i, place
        )

    def feed_wait(turn, k):
        part = m_all.at[turn, k]
        remote(
            part, part, pass_send.at[0, 0], feed_recv.at[turn, k], partner, place
        ).wait_recv()

    def pass_on(turn, k):
        return remote(
            m_all.at[turn, k], m_all.at[turn, k + 1], pass_send.at[turn, k],
            feed_recv.at[turn, k + 1], site, at(-1),
        )

    def pass_first(turn):
        return remote(
            ring.at[0, parity], m_all.at[turn, 1], pass_send.at[turn, 0],
            feed_recv.at[turn, 1], site, at(-1),
        )

    def start(blocks, target, slot):
        low = blocks[0]
        mid = blocks[1:3].reshape(2 * width, width)
        top = blocks[3]
        step = 32
        total = jnp.zeros((8, width), F32)
        for row in range(0, width, step):
            g0 = nt(low[row : row + step], low)
            g1 = nt(mid[row : row + step], mid)
            g2 = nt(mid[width + row : width + row + step], mid)
            g3 = nt(top[row : row + step], top)
            parts = (g0, g1[:, :width], g1[:, width:], g2[:, :width], g2[:, width:], g3)
            parts = [x.reshape(step // 8, 8, width) for x in parts]
            for w in range(channels):
                block = parts[0] * coef[0, w][None]
                for i in range(1, len(PAIRS)):
                    block = block + parts[i] * coef[i, w][None]
                target[w, row : row + step, :] = block.reshape(step, width).astype(BF16)
                small = block * SMALL
                total = total + jnp.sum(small * small, axis=0)
        squares[slot, 0] += total

    def last_copy(i, pair):
        part = r_all.at[3, i, 0, pl.ds(2 * pair, 2)]
        return remote(part, part, last_send.at[pair], last_recv.at[i, pair], end, place)

    def advance(turn, j):
        prev = turn - 1
        low = m_all[turn, j, 0]
        mid = m_all[turn, j, 1:3].reshape(2 * width, width)
        top = m_all[turn, j, 3]
        step = 32

        def pairs(x):
            y = x.reshape(channels, step // 8, 8, width)
            cut = lambda i: y[:, i].reshape(channels * 8, width)
            return [
                jnp.concatenate([cut(2 * j), cut(2 * j + 1)], axis=1).astype(BF16)
                for j in range(step // 16)
            ]

        k_low, k_mid, k_top = mix_low[prev], mix_mid[prev], mix_top[prev]
        for row in range(0, width, step):
            def rows_of(which, slot):
                rows = r_all[prev, which, slot, :, row : row + step, :]
                return rows.reshape(channels * step, width)

            x0 = pairs(nt(rows_of(parity, j), low))
            x12 = nt(rows_of(1 - parity, j + parity), mid)
            x1, x2 = pairs(x12[:, :width]), pairs(x12[:, width:])
            x3 = pairs(nt(rows_of(parity, j + 1), top))
            for i in range(step // 16):
                y0 = nn(k_low, x0[i])
                y12 = nn(k_mid, jnp.concatenate([x1[i], x2[i]], axis=0))
                y3 = nn(k_top, x3[i])
                for s, y in ((0, y0), (1, y12[: channels * 8]), (2, y12[channels * 8 :]), (3, y3)):
                    z = y.reshape(channels, 8, 2 * width)
                    at_row = s * width + row + 16 * i
                    for w in range(channels):
                        both = jnp.concatenate([z[w, :, :width], z[w, :, width:]], axis=0)
                        lane = (w % 2) * width
                        mixed[w // 2, at_row : at_row + 16, lane : lane + width] = both.astype(BF16)
        wide = jnp.concatenate([low, mid[:width], mid[width:], top], axis=1)
        total = jnp.zeros((8, 2 * width), F32)
        for pair in range(channels // 2):
            block = nn(wide, mixed[pair])
            r_all[turn, parity, j, 2 * pair] = block[:, :width].astype(BF16)
            r_all[turn, parity, j, 2 * pair + 1] = block[:, width:].astype(BF16)
            small = block * SMALL
            total = total + jnp.sum((small * small).reshape(width // 8, 8, 2 * width), axis=0)
        slot = (j >= 1).astype(jnp.int32)
        squares[slot, turn] += total[:, :width] + total[:, width:]

    def swap(turn, j):
        part = r_all.at[turn, parity, j]
        return remote(part, part, swap_send.at[turn, j], swap_recv.at[turn, j], partner, place)

    def swap_wait(turn, j):
        part = r_all.at[turn, 1 - parity, j]
        remote(
            part, part, swap_send.at[turn, j], swap_recv.at[turn, j], partner, place
        ).wait_recv()

    def swaps(turn, j):
        even = (parity == 0) & ((j >= 1) | (turn == 1))
        odd = (parity == 1) & (j <= 2 - turn)
        return (turn < 3) & (even | odd)

    def tell(i):
        for step in (ROUNDS[i], -ROUNDS[i]):
            pl.semaphore_signal(
                round_sem.at[i], inc=1, device_id=(site, at(step)), device_id_type=MESH
            )

    def told(i):
        pl.semaphore_wait(round_sem.at[i], 2)

    targets = (end, hub, hub + 1, far)

    def sum_copy(kind, step):
        return remote(
            mine, heard.at[parity * places + place], sum_send.at[kind, step], sum_recv,
            targets[kind], at(step),
        )

    def sum_self(kind, step):
        return (step == 0) & (kind == parity + 1)

    @pl.when(role == 2)
    def _():
        pl.semaphore_wait(barrier, 4)

        @pl.loop(0, REACH)
        def _(k):
            for i in range(held):
                @pl.when(k > 0)
                def _():
                    ring_wait(k, i)

                @pl.when(k < REACH - 1)
                def _():
                    ring_copy(k, i).start()

                feed(0, k, i, ring.at[k, i], feed_send.at[k, i]).start()

        edge_of(table_of(SITES - 1, mpo_ref, mask_ref, table), channels, coef)
        squares[...] = jnp.zeros_like(squares)

        @pl.loop(0, held)
        def _(i):
            start(ring.at[0, i], r_all.at[0, i, 0], 1)

    @pl.when(role == 3)
    def _():
        pl.semaphore_wait(barrier, 2)
        for i in range(held):
            feed(3, 0, i, ring.at[0, i], feed_send.at[0, i]).start()

    @pl.when(works)
    def _():
        home = 2 - parity
        pl.semaphore_wait(barrier, 5)
        tell(0)
        feed(home, 0, 1 - parity, ring.at[0, 1 - parity], feed_send.at[0, 0]).start()
        pass_first(home).start()
        m_all[home, 0] = ring[0, parity]
        edge_of(table_of(SITES - 1, mpo_ref, mask_ref, table), channels, coef)
        squares[...] = jnp.zeros_like(squares)
        feed_wait(1 + parity, 0)
        pass_on(1 + parity, 0).start()
        told(0)
        tell(1)
        for turn in range(1, SITES):
            found = table_of(SITES - 1 - turn, mpo_ref, mask_ref, table)
            mix_low[turn - 1] = spread(found, channels, 0, 1)
            mix_mid[turn - 1] = spread(found, channels, 1, 2)
            mix_top[turn - 1] = spread(found, channels, 3, 1)
        feed_wait(1, 1)
        pass_on(1, 1).start()
        told(1)
        tell(2)

        @pl.loop(0, REACH)
        def _(k):
            feed_wait(0, k)
            start(m_all.at[0, k], r_all.at[0, parity, k], (k >= 1).astype(jnp.int32))

            @pl.when(swaps(0, k))
            def _():
                swap(0, k).start()

            @pl.loop(1, k + 1)
            def _(t):
                @pl.when(k == REACH - 1)
                def _():
                    feed_wait(t, k - t)

                swap_wait(t - 1, k - t + parity)
                advance(t, k - t)

                @pl.when(swaps(t, k - t))
                def _():
                    swap(t, k - t).start()

                @pl.when(t == 3)
                def _():
                    for pair in range(channels // 2):
                        last_copy(parity, pair).start()

            @pl.when(k == 1)
            def _():
                told(2)
                tell(3)

        lane = ids(1, width, 1)
        row = jnp.zeros((1, width), F32)
        for t in range(SITES):
            row = row + jnp.where(lane == t, jnp.sum(squares[0, t]), 0.0)
        mine[...] = row
        heard[parity * places + place] = row
        told(3)

        for kind in range(4):
            @pl.loop(0, places)
            def _(step):
                @pl.when(jnp.logical_not(sum_self(kind, step)))
                def _():
                    sum_copy(kind, step).start()

    def heard_all(count):
        part = heard.at[pl.ds(0, count)]
        remote(part, part, sum_send.at[0, 0], sum_recv, site, at(1)).wait_recv()

    @pl.when(role == 3)
    def _():
        for i in range(held):
            for pair in range(channels // 2):
                last_copy(i, pair).wait_recv()

    @pl.when(role == 1)
    def _():
        swap_wait(1, 0)

    @pl.when(works)
    def _():
        heard_all(2 * places - 1)

    @pl.when(role >= 2)
    def _():
        heard_all(2 * places)

    turn = jnp.where(role == 3, 3, 2 - role)
    sums = jnp.sum(heard[...].reshape(2 * places, width), axis=0, keepdims=True)
    entries = float(places * held * channels * width * width)
    unit = jnp.ones((1, 1), F32)
    chosen = unit
    for t in range(SITES):
        square = sums[:, t : t + 1] * (1.0 / (SMALL * SMALL * entries)) * unit * unit
        unit = unit * lax.rsqrt(square + EPSILON)
        chosen = jnp.where(turn == t, unit, chosen)
    scale_ref[...] = jnp.broadcast_to(chosen, scale_ref.shape)
    for i in range(held):
        out_ref[i] = r_all[turn, i, 0]

    @pl.when(works)
    def _():
        home = 2 - parity
        feed(home, 0, 1 - parity, ring.at[0, 1 - parity], feed_send.at[0, 0]).wait_send()
        for t, k in ((1, 0), (1, 1), (2, 0)):
            pass_on(t, k).wait_send()
        for t in range(SITES - 1):
            for j in range(REACH - t):
                @pl.when(swaps(t, j))
                def _():
                    swap(t, j).wait_send()
        for pair in range(channels // 2):
            last_copy(parity, pair).wait_send()
        for kind in range(4):
            @pl.loop(0, places)
            def _(step):
                @pl.when(jnp.logical_not(sum_self(kind, step)))
                def _():
                    sum_copy(kind, step).wait_send()

    @pl.when(role == 2)
    def _():
        for k in range(REACH):
            for i in range(held):
                if k < REACH - 1:
                    ring_copy(k, i).wait_send()
                feed(0, k, i, ring.at[k, i], feed_send.at[k, i]).wait_send()

    @pl.when(role == 3)
    def _():
        for i in range(held):
            feed(3, 0, i, ring.at[0, i], feed_send.at[0, i]).wait_send()


def scaled(in_ref, scale_ref, out_ref, final, done_sem):
    channels = final.shape[1]
    factor = scale_ref[0:1, :].reshape(1, 1, final.shape[-1])

    def put(w):
        return pltpu.make_async_copy(final.at[:, w], out_ref.at[:, w], done_sem.at[w])

    for w in range(channels):
        final[:, w] = (in_ref[:, w].astype(F32) * factor).astype(BF16)
        put(w).start()
    for w in range(channels):
        put(w).wait()


def on_device(mps, mpo, mpo_mask, sector_size, pair_live):
    places = lax.axis_size("tensor")
    held, width = mps.shape[1], mps.shape[-1]
    channels = mpo.shape[1]
    vmem, dma = pltpu.VMEM, pltpu.SemaphoreType.DMA
    in_vmem, in_smem = pl.BlockSpec(memory_space=pltpu.VMEM), pl.BlockSpec(memory_space=pltpu.SMEM)
    result = (held, channels, width, width)
    environment, scale = pl.pallas_call(
        kernel,
        out_shape=(
            jax.ShapeDtypeStruct(result, BF16),
            jax.ShapeDtypeStruct((8, width), F32),
        ),
        in_specs=[pl.BlockSpec(memory_space=pl.ANY), in_vmem, in_vmem, in_smem, in_smem],
        out_specs=(in_vmem, in_vmem),
        scratch_shapes=[
            vmem((held, PHYS, width, width), BF16),
            vmem((REACH, held, PHYS, width, width), BF16),
            vmem((SITES, REACH, PHYS, width, width), BF16),
            vmem((SITES, 2, REACH, channels, width, width), BF16),
            vmem((SITES - 1, channels * 8, channels * 8), BF16),
            vmem((SITES - 1, channels * 16, channels * 16), BF16),
            vmem((SITES - 1, channels * 8, channels * 8), BF16),
            vmem((len(PAIRS), channels, 8, width), F32),
            vmem((channels * PHYS * PHYS, width), F32),
            vmem((channels // 2, PHYS * width, 2 * width), BF16),
            vmem((2, SITES, 8, width), F32),
            vmem((1, width), F32),
            vmem((2 * places, 1, width), F32),
            dma,
            dma((REACH, held)),
            dma((REACH, held)),
            dma((REACH, held)),
            dma((SITES, REACH)),
            dma((SITES, REACH)),
            dma((SITES, REACH)),
            dma((SITES, REACH)),
            dma((channels // 2,)),
            dma((held, channels // 2)),
            dma((SITES, places)),
            dma,
            pltpu.SemaphoreType.REGULAR((len(ROUNDS),)),
        ],
        compiler_params=pltpu.CompilerParams(
            collective_id=0, has_side_effects=True, vmem_limit_bytes=48 * 1024 * 1024
        ),
    )(
        mps[0],
        jnp.transpose(mpo, (0, 1, 3, 4, 2)),
        jnp.transpose(mpo_mask, (1, 0, 2)),
        sector_size,
        pair_live,
    )
    return pl.pallas_call(
        scaled,
        out_shape=jax.ShapeDtypeStruct(result, BF16),
        in_specs=[in_vmem, in_vmem],
        out_specs=pl.BlockSpec(memory_space=pl.ANY),
        scratch_shapes=[vmem(result, BF16), dma((channels,))],
    )(environment, scale)[None]


def solution(mesh):
    in_specs = (
        P("site", "tensor", None, None, None),
        P(),
        P(),
        P("site", "tensor"),
        P("site", "tensor", None),
    )
    out_specs = P("site", "tensor", None, None, None)
    return jax.shard_map(
        on_device, mesh=mesh, in_specs=in_specs, out_specs=out_specs, check_vma=False
    )
```

time: 193 us -> 54.4 us (0.28)
  the two profiles are of different devices: /device:TPU:9 before, /device:TPU:1 now
where the time goes in v2:
time: 54.4 us; the launch traced here: 54.1 us
  Pallas kernels  49.4 us (91%)
  local copies, waits for them, and re-layouts  4.69 us (9%)
    pallas_call x1, Pallas kernels, on_device(): pl.pallas_call(kernel, out_shape=(jax.ShapeDtypeStruct(result, BF16), jax...  47.4 us
    unnamed x14, local copies, waits for them, and re-layouts  4.69 us
    pallas_call x1, Pallas kernels, on_device(): pl.pallas_call(scaled, out_shape=jax.ShapeDtypeStruct(result, BF16), in_s...  2.01 us

profile of v2, /device:TPU:1, one launch (start us, length us, event | category | flops | bytes accessed | tf_op | source)
XLA Modules:
  0.0 54.1 jit_solution(9425699836754377778)
XLA Ops:
  0.0 0.0 copy-start.5
  0.0 0.0 copy-start.6
  0.0 0.7 %copy-done.5 = s32[1,2,3]{2,1,0:T(2,128)S(1)} copy-done((s32[1,2,3]{2,1,0:T(2,128)S(1)}, s32[1,2,3]{2,1,0:T(2,128)}, u32[]{:S(2)}) %copy-start.5) | copy-done | bytes 48
  0.7 0.0 copy-done.6
  0.7 0.0 copy-start.1
  0.7 0.9 %copy-done.1 = bf16[1,2,4,128,128]{4,3,2,1,0:T(8,128)(2,1)S(1)} copy-done((bf16[1,2,4,128,128]{4,3,2,1,0:T(8,128)(2,1)S(1)}, bf16[1,2,4,128,128]{4,3,2,1,0:T(8,128)(2,1)}, u32[]{:S(2)}) %copy-start.1) | copy-done | bytes 262168
  1.6 0.0 copy-start.2
  1.6 0.9 %copy-done.2 = bf16[4,10,10,4,4]{2,4,3,1,0:T(4,128)(2,1)S(1)} copy-done((bf16[4,10,10,4,4]{2,4,3,1,0:T(4,128)(2,1)S(1)}, bf16[4,10,10,4,4]{2,4,3,1,0:T(4,128)(2,1)}, u32[]{:S(2)}) %copy-start.2) | copy-done | bytes 12824
  2.5 0.0 copy-start.3
  2.6 0.7 %copy-done.3 = s32[4,10,10]{2,0,1:T(4,128)S(1)} copy-done((s32[4,10,10]{2,0,1:T(4,128)S(1)}, s32[4,10,10]{2,0,1:T(4,128)}, u32[]{:S(2)}) %copy-start.3) | copy-done | bytes 1624
  3.3 47.4 %shard_map.55 = (bf16[2,10,128,128]{3,2,1,0:T(8,128)(2,1)S(1)}, f32[8,128]{1,0:T(8,128)S(1)}) custom-call(bf16[2,4,128,128]{3,2,1,0:T(8,128)(2,1)S(1)} %bitcast.4, bf16[4,10,4,4,10]{4,3,2,1,0:T(4,128)(2,1)S(1)} %bitcast.5, s32[10,4,10]{2,1,0:T(4,128)S(1)} %bitcast.6, s32[1,2]{1,0:T(1,128)S(1)} %copy-done.6, s32[1,2,3]{2,1,0:T(2,128)S(1)} %copy-done.5), custom_call_target="tpu_custom_call" | custom-call | tf_op jit(solution)/shard_map/pallas_call | solution.py:467
  50.7 0.0 copy-start
  50.7 0.8 %copy-done = bf16[2,10,128,128]{3,2,1,0:T(8,128)(2,1)} copy-done((bf16[2,10,128,128]{3,2,1,0:T(8,128)(2,1)}, bf16[2,10,128,128]{3,2,1,0:T(8,128)(2,1)S(1)}, u32[]{:S(2)}) %copy-start) | copy-done | bytes 655384
  51.5 0.0 copy-start.4
  51.5 0.6 %copy-done.4 = f32[8,128]{1,0:T(8,128)} copy-done((f32[8,128]{1,0:T(8,128)}, f32[8,128]{1,0:T(8,128)S(1)}, u32[]{:S(2)}) %copy-start.4) | copy-done | bytes 4120
  52.1 2.0 %shard_map.56 = bf16[2,10,128,128]{3,2,1,0:T(8,128)(2,1)} custom-call(bf16[2,10,128,128]{3,2,1,0:T(8,128)(2,1)} %copy-done, f32[8,128]{1,0:T(8,128)} %copy-done.4), custom_call_target="tpu_custom_call" | custom-call | tf_op jit(solution)/shard_map/pallas_call | solution.py:513
Async XLA Ops:
  0.0 0.7 %copy-start.5 = (s32[1,2,3]{2,1,0:T(2,128)S(1)}, s32[1,2,3]{2,1,0:T(2,128)}, u32[]{:S(2)}) copy-start(s32[1,2,3]{2,1,0:T(2,128)} %live_ref.1) | copy-start | bytes 76
  0.0 0.7 %copy-start.6 = (s32[1,2]{1,0:T(1,128)S(1)}, s32[1,2]{1,0:T(1,128)}, u32[]{:S(2)}) copy-start(s32[1,2]{1,0:T(1,128)} %size_ref.1) | copy-start | bytes 28
  0.7 1.0 %copy-start.1 = (bf16[1,2,4,128,128]{4,3,2,1,0:T(8,128)(2,1)S(1)}, bf16[1,2,4,128,128]{4,3,2,1,0:T(8,128)(2,1)}, u32[]{:S(2)}) copy-start(bf16[1,2,4,128,128]{4,3,2,1,0:T(8,128)(2,1)} %param.5) | copy-start | bytes 786436
  1.6 0.9 %copy-start.2 = (bf16[4,10,10,4,4]{2,4,3,1,0:T(4,128)(2,1)S(1)}, bf16[4,10,10,4,4]{2,4,3,1,0:T(4,128)(2,1)}, u32[]{:S(2)}) copy-start(bf16[4,10,10,4,4]{2,4,3,1,0:T(4,128)(2,1)} %param.6) | copy-start | bytes 38404
  2.5 0.7 %copy-start.3 = (s32[4,10,10]{2,0,1:T(4,128)S(1)}, s32[4,10,10]{2,0,1:T(4,128)}, u32[]{:S(2)}) copy-start(s32[4,10,10]{2,0,1:T(4,128)} %param.7) | copy-start | bytes 4804
  50.7 0.8 %copy-start = (bf16[2,10,128,128]{3,2,1,0:T(8,128)(2,1)}, bf16[2,10,128,128]{3,2,1,0:T(8,128)(2,1)S(1)}, u32[]{:S(2)}) copy-start(bf16[2,10,128,128]{3,2,1,0:T(8,128)(2,1)S(1)} %get-tuple-element.7.in_ref) | copy-start | bytes 1966084
  51.5 0.6 %copy-start.4 = (f32[8,128]{1,0:T(8,128)}, f32[8,128]{1,0:T(8,128)S(1)}, u32[]{:S(2)}) copy-start(f32[8,128]{1,0:T(8,128)S(1)} %get-tuple-element.8.scale_ref) | copy-start | bytes 12292

commit v3 on v2

--- a/solution.py
+++ b/solution.py
@@ -75,10 +75,10 @@
 
 
 def kernel(
-    m_ref, mpo_ref, mask_ref, size_ref, live_ref, out_ref, scale_ref,
-    raw, ring, m_all, r_all, mix_low, mix_mid, mix_top, coef, table, mixed, squares, mine, heard,
-    raw_sem, ring_send, ring_recv, feed_send, feed_recv, pass_send, swap_send, swap_recv,
-    last_send, last_recv, sum_send, sum_recv, round_sem,
+    m_ref, mpo_in, mask_in, size_in, live_in, out_ref, scale_ref,
+    mpo_ref, mask_ref, size_ref, live_ref, raw, ring, m_all, r_all, mix_low, mix_mid, mix_top, coef, table, mixed, squares, mine, heard,
+    load_sem, ring_send, ring_recv, feed_send, feed_recv, pass_send, swap_send, swap_recv,
+    sum_send, sum_recv, round_sem,
 ):
     site, place = lax.axis_index("site"), lax.axis_index("tensor")
     sites, places = lax.axis_size("site"), lax.axis_size("tensor")
@@ -95,8 +95,15 @@
     def at(step):
         return lax.rem(place + step + places, places)
 
-    load = pltpu.make_async_copy(m_ref, raw, raw_sem)
-    load.start()
+    loads = [
+        pltpu.make_async_copy(src, dst, load_sem.at[i])
+        for i, (src, dst) in enumerate((
+            (m_ref, raw), (size_in, size_ref), (live_in, live_ref),
+            (mpo_in, mpo_ref), (mask_in, mask_ref),
+        ))
+    ]
+    for load in loads:
+        load.start()
     barrier = pltpu.get_barrier_semaphore()
 
     def greet(*targets):
@@ -115,7 +122,8 @@
     def _():
         greet((hub, place), (hub + 1, place))
 
-    load.wait()
+    for load in loads:
+        load.wait()
     for i in range(held):
         sector = place * held + i
         for s in range(PHYS):
@@ -131,16 +139,26 @@
             device_id=(site_to, place_to), device_id_type=MESH,
         )
 
-    def ring_copy(k, i):
-        return remote(
-            ring.at[k, i], ring.at[k + 1, i], ring_send.at[k, i], ring_recv.at[k + 1, i],
+    def half(k, i, h):
+        return ring.at[k, i, pl.ds(2 * h, 2)]
+
+    def ring_copy(k, i, h):
+        return remote(
+            half(k, i, h), half(k + 1, i, h), ring_send.at[k, i, h], ring_recv.at[k + 1, i, h],
             site, at(-1),
         )
 
-    def ring_wait(k, i):
+    def ring_wait(k, i, h):
         remote(
-            ring.at[k, i], ring.at[k, i], ring_send.at[0, 0], ring_recv.at[k, i], site, at(-1)
+            half(k, i, h), half(k, i, h), ring_send.at[0, 0, 0], ring_recv.at[k, i, h],
+            site, at(-1),
         ).wait_recv()
+
+    def feed_half(k, i, h):
+        return remote(
+            half(k, i, h), m_all.at[0, k, pl.ds(2 * h, 2)], feed_send.at[k, i],
+            feed_recv.at[0, k], hub + i, place,
+        )
 
     def feed(turn, k, i, source, send):
         return remote(
@@ -187,9 +205,21 @@
                 total = total + jnp.sum(small * small, axis=0)
         squares[slot, 0] += total
 
-    def last_copy(i, pair):
-        part = r_all.at[3, i, 0, pl.ds(2 * pair, 2)]
-        return remote(part, part, last_send.at[pair], last_recv.at[i, pair], end, place)
+    def swap_part(turn, j, part):
+        last = turn == SITES - 1
+        arrival = jnp.where(last, parity, j)
+        return remote(
+            part, part, swap_send.at[turn, j], swap_recv.at[turn, arrival],
+            jnp.where(last, end, partner), place,
+        )
+
+    def swap(turn, j):
+        return swap_part(turn, j, r_all.at[turn, parity, j])
+
+    def swap_pair(turn, j, pair):
+        @pl.when(swaps(turn, j))
+        def _():
+            swap_part(turn, j, r_all.at[turn, parity, j, pl.ds(2 * pair, 2)]).start()
 
     def advance(turn, j):
         prev = turn - 1
@@ -235,12 +265,11 @@
             r_all[turn, parity, j, 2 * pair + 1] = block[:, width:].astype(BF16)
             small = block * SMALL
             total = total + jnp.sum((small * small).reshape(width // 8, 8, 2 * width), axis=0)
+            if pair > 0:
+                swap_pair(turn, j, pair - 1)
         slot = (j >= 1).astype(jnp.int32)
         squares[slot, turn] += total[:, :width] + total[:, width:]
-
-    def swap(turn, j):
-        part = r_all.at[turn, parity, j]
-        return remote(part, part, swap_send.at[turn, j], swap_recv.at[turn, j], partner, place)
+        swap_pair(turn, j, channels // 2 - 1)
 
     def swap_wait(turn, j):
         part = r_all.at[turn, 1 - parity, j]
@@ -251,7 +280,7 @@
     def swaps(turn, j):
         even = (parity == 0) & ((j >= 1) | (turn == 1))
         odd = (parity == 1) & (j <= 2 - turn)
-        return (turn < 3) & (even | odd)
+        return (turn == 3) | even | odd
 
     def tell(i):
         for step in (ROUNDS[i], -ROUNDS[i]):
@@ -280,15 +309,16 @@
         @pl.loop(0, REACH)
         def _(k):
             for i in range(held):
-                @pl.when(k > 0)
-                def _():
-                    ring_wait(k, i)
-
-                @pl.when(k < REACH - 1)
-                def _():
-                    ring_copy(k, i).start()
-
-                feed(0, k, i, ring.at[k, i], feed_send.at[k, i]).start()
+                for h in range(2):
+                    @pl.when(k > 0)
+                    def _():
+                        ring_wait(k, i, h)
+
+                    @pl.when(k < REACH - 1)
+                    def _():
+                        ring_copy(k, i, h).start()
+
+                    feed_half(k, i, h).start()
 
         edge_of(table_of(SITES - 1, mpo_ref, mask_ref, table), channels, coef)
         squares[...] = jnp.zeros_like(squares)
@@ -345,15 +375,6 @@
                 swap_wait(t - 1, k - t + parity)
                 advance(t, k - t)
 
-                @pl.when(swaps(t, k - t))
-                def _():
-                    swap(t, k - t).start()
-
-                @pl.when(t == 3)
-                def _():
-                    for pair in range(channels // 2):
-                        last_copy(parity, pair).start()
-
             @pl.when(k == 1)
             def _():
                 told(2)
@@ -381,8 +402,10 @@
     @pl.when(role == 3)
     def _():
         for i in range(held):
-            for pair in range(channels // 2):
-                last_copy(i, pair).wait_recv()
+            part = r_all.at[3, i, 0]
+            remote(
+                part, part, swap_send.at[3, 0], swap_recv.at[3, i], hub + i, place
+            ).wait_recv()
 
     @pl.when(role == 1)
     def _():
@@ -415,13 +438,11 @@
         feed(home, 0, 1 - parity, ring.at[0, 1 - parity], feed_send.at[0, 0]).wait_send()
         for t, k in ((1, 0), (1, 1), (2, 0)):
             pass_on(t, k).wait_send()
-        for t in range(SITES - 1):
+        for t in range(SITES):
             for j in range(REACH - t):
                 @pl.when(swaps(t, j))
                 def _():
                     swap(t, j).wait_send()
-        for pair in range(channels // 2):
-            last_copy(parity, pair).wait_send()
         for kind in range(4):
             @pl.loop(0, places)
             def _(step):
@@ -433,8 +454,9 @@
     def _():
         for k in range(REACH):
             for i in range(held):
-                if k < REACH - 1:
-                    ring_copy(k, i).wait_send()
+                for h in range(2):
+                    if k < REACH - 1:
+                        ring_copy(k, i, h).wait_send()
                 feed(0, k, i, ring.at[k, i], feed_send.at[k, i]).wait_send()
 
     @pl.when(role == 3)
@@ -462,7 +484,7 @@
     held, width = mps.shape[1], mps.shape[-1]
     channels = mpo.shape[1]
     vmem, dma = pltpu.VMEM, pltpu.SemaphoreType.DMA
-    in_vmem, in_smem = pl.BlockSpec(memory_space=pltpu.VMEM), pl.BlockSpec(memory_space=pltpu.SMEM)
+    in_vmem, in_hbm = pl.BlockSpec(memory_space=pltpu.VMEM), pl.BlockSpec(memory_space=pltpu.HBM)
     result = (held, channels, width, width)
     environment, scale = pl.pallas_call(
         kernel,
@@ -470,9 +492,13 @@
             jax.ShapeDtypeStruct(result, BF16),
             jax.ShapeDtypeStruct((8, width), F32),
         ),
-        in_specs=[pl.BlockSpec(memory_space=pl.ANY), in_vmem, in_vmem, in_smem, in_smem],
+        in_specs=[in_hbm] * 5,
         out_specs=(in_vmem, in_vmem),
         scratch_shapes=[
+            vmem((SITES, channels, PHYS, PHYS, channels), BF16),
+            vmem((channels, SITES, channels), jnp.int32),
+            pltpu.SMEM((1, held), jnp.int32),
+            pltpu.SMEM((1, held, 3), jnp.int32),
             vmem((held, PHYS, width, width), BF16),
             vmem((REACH, held, PHYS, width, width), BF16),
             vmem((SITES, REACH, PHYS, width, width), BF16),
@@ -486,16 +512,14 @@
             vmem((2, SITES, 8, width), F32),
             vmem((1, width), F32),
             vmem((2 * places, 1, width), F32),
-            dma,
-            dma((REACH, held)),
-            dma((REACH, held)),
+            dma((5,)),
+            dma((REACH, held, 2)),
+            dma((REACH, held, 2)),
             dma((REACH, held)),
             dma((SITES, REACH)),
             dma((SITES, REACH)),
             dma((SITES, REACH)),
             dma((SITES, REACH)),
-            dma((channels // 2,)),
-            dma((held, channels // 2)),
             dma((SITES, places)),
             dma,
             pltpu.SemaphoreType.REGULAR((len(ROUNDS),)),
@@ -504,11 +528,16 @@
             collective_id=0, has_side_effects=True, vmem_limit_bytes=48 * 1024 * 1024
         ),
     )(
-        mps[0],
-        jnp.transpose(mpo, (0, 1, 3, 4, 2)),
-        jnp.transpose(mpo_mask, (1, 0, 2)),
-        sector_size,
-        pair_live,
+        *[
+            pltpu.with_memory_space_constraint(x, pltpu.HBM)
+            for x in (
+                mps[0],
+                jnp.transpose(mpo, (0, 1, 3, 4, 2)),
+                jnp.transpose(mpo_mask, (1, 0, 2)),
+                sector_size,
+                pair_live,
+            )
+        ]
     )
     return pl.pallas_call(
         scaled,
@@ -516,6 +545,7 @@
         in_specs=[in_vmem, in_vmem],
         out_specs=pl.BlockSpec(memory_space=pl.ANY),
         scratch_shapes=[vmem(result, BF16), dma((channels,))],
+        compiler_params=pltpu.CompilerParams(vmem_limit_bytes=4 * 1024 * 1024),
     )(environment, scale)[None]
 
 

time: 54.4 us -> 50.4 us (0.926)
  local copies, waits for them, and re-layouts: 4.69 us -> 0 us
  Pallas kernels: 49.4 us -> 50.3 us
    unnamed x14 -> x0, local copies, waits for them, and re-layouts: 4.69 us -> none
    pallas_call x1, Pallas kernels: 47.4 us -> 49.4 us  [on_device(): pl.pallas_call(kernel, out_shape=(jax.ShapeDtypeStruct(result, BF16), jax...]
    pallas_call x1, Pallas kernels: 2.01 us -> 0.92 us  [on_device(): pl.pallas_call(scaled, out_shape=jax.ShapeDtypeStruct(result, BF16), in_s...]
where the time goes in v3:
time: 50.4 us; the launch traced here: 50.3 us
  Pallas kernels  50.3 us (100%)
    pallas_call x1, Pallas kernels, on_device(): pl.pallas_call(kernel, out_shape=(jax.ShapeDtypeStruct(result, BF16), jax...  49.4 us

profile of v3, /device:TPU:1, one launch (start us, length us, event | category | flops | bytes accessed | tf_op | source)
XLA Modules:
  0.0 50.3 jit_solution(8009167372938009093)
XLA Ops:
  0.0 49.4 %shard_map.55 = (bf16[2,10,128,128]{3,2,1,0:T(8,128)(2,1)S(1)}, f32[8,128]{1,0:T(8,128)S(1)}) custom-call(bf16[2,4,128,128]{3,2,1,0:T(8,128)(2,1)} %bitcast.4, bf16[4,10,4,4,10]{4,3,2,1,0:T(4,128)(2,1)} %bitcast.5, s32[10,4,10]{2,1,0:T(4,128)} %bitcast.6, s32[1,2]{1,0:T(1,128)} %size_in.1, s32[1,2,3]{2,1,0:T(2,128)} %live_in.1), custom_call_target="tpu_custom_call" | custom-call | tf_op jit(solution)/shard_map/pallas_call | solution.py:489
  49.4 0.9 %shard_map.56 = bf16[2,10,128,128]{3,2,1,0:T(8,128)(2,1)} custom-call(bf16[2,10,128,128]{3,2,1,0:T(8,128)(2,1)S(1)} %get-tuple-element.7.in_ref, f32[8,128]{1,0:T(8,128)S(1)} %get-tuple-element.8.scale_ref), custom_call_target="tpu_custom_call" | custom-call | tf_op jit(solution)/shard_map/pallas_call | solution.py:542

commit v4 on v3

--- a/solution.py
+++ b/solution.py
@@ -76,7 +76,7 @@
 
 def kernel(
     m_ref, mpo_in, mask_in, size_in, live_in, out_ref, scale_ref,
-    mpo_ref, mask_ref, size_ref, live_ref, raw, ring, m_all, r_all, mix_low, mix_mid, mix_top, coef, table, mixed, squares, mine, heard,
+    mpo_ref, mask_ref, size_ref, live_ref, raw, ring, m_all, r_all, mix_low, mix_mid, mix_top, coef, table, mixed, partial, squares, mine, heard,
     load_sem, ring_send, ring_recv, feed_send, feed_recv, pass_send, swap_send, swap_recv,
     sum_send, sum_recv, round_sem,
 ):
@@ -112,17 +112,19 @@
 
     @pl.when(works)
     def _():
-        greet((far, place), (end, place), (partner, place), (site, at(1)), (site, at(-1)))
+        greet((far, place), (far, at(1)), (end, place), (partner, place))
+        greet((site, at(1)), (site, at(-1)))
 
     @pl.when(role == 2)
     def _():
-        greet((hub, place), (hub + 1, place), (site, at(1)), (site, at(-1)))
+        greet((hub, place), (hub + 1, place), (hub, at(-1)), (hub + 1, at(-1)))
+        greet((site, at(1)), (site, at(-1)))
 
     @pl.when(role == 3)
     def _():
         greet((hub, place), (hub + 1, place))
 
-    for load in loads:
+    for load in loads[:3]:
         load.wait()
     for i in range(held):
         sector = place * held + i
@@ -133,6 +135,10 @@
             block = jnp.where(ids(width, width, 0) < bound, raw[i, s].astype(F32), 0.0)
             ring[0, i, s] = block.astype(BF16)
 
+    def load_weights():
+        for load in loads[3:]:
+            load.wait()
+
     def remote(src, dst, send, recv, site_to, place_to):
         return pltpu.make_async_remote_copy(
             src_ref=src, dst_ref=dst, send_sem=send, recv_sem=recv,
@@ -153,6 +159,12 @@
             half(k, i, h), half(k, i, h), ring_send.at[0, 0, 0], ring_recv.at[k, i, h],
             site, at(-1),
         ).wait_recv()
+
+    def feed_far(i, h):
+        return remote(
+            half(2, i, h), m_all.at[0, REACH - 1, pl.ds(2 * h, 2)], feed_send.at[REACH - 1, i],
+            feed_recv.at[0, REACH - 1], hub + i, at(-1),
+        )
 
     def feed_half(k, i, h):
         return remote(
@@ -217,11 +229,11 @@
         return swap_part(turn, j, r_all.at[turn, parity, j])
 
     def swap_pair(turn, j, pair):
-        @pl.when(swaps(turn, j))
+        @pl.when(swaps(turn, j) & (turn < SITES - 1))
         def _():
             swap_part(turn, j, r_all.at[turn, parity, j, pl.ds(2 * pair, 2)]).start()
 
-    def advance(turn, j):
+    def advance(turn, j, parts=(0, 1, 2), first=True, last=True):
         prev = turn - 1
         low = m_all[turn, j, 0]
         mid = m_all[turn, j, 1:3].reshape(2 * width, width)
@@ -236,40 +248,56 @@
                 for j in range(step // 16)
             ]
 
-        k_low, k_mid, k_top = mix_low[prev], mix_mid[prev], mix_top[prev]
         for row in range(0, width, step):
             def rows_of(which, slot):
                 rows = r_all[prev, which, slot, :, row : row + step, :]
                 return rows.reshape(channels * step, width)
 
-            x0 = pairs(nt(rows_of(parity, j), low))
-            x12 = nt(rows_of(1 - parity, j + parity), mid)
-            x1, x2 = pairs(x12[:, :width]), pairs(x12[:, width:])
-            x3 = pairs(nt(rows_of(parity, j + 1), top))
+            def put(s, i, y):
+                z = y.reshape(channels, 8, 2 * width)
+                at_row = s * width + row + 16 * i
+                for w in range(channels):
+                    both = jnp.concatenate([z[w, :, :width], z[w, :, width:]], axis=0)
+                    lane = (w % 2) * width
+                    mixed[w // 2, at_row : at_row + 16, lane : lane + width] = both.astype(BF16)
+
+            if 0 in parts:
+                x0 = pairs(nt(rows_of(parity, j), low))
+            if 1 in parts:
+                x12 = nt(rows_of(1 - parity, j + parity), mid)
+                x1, x2 = pairs(x12[:, :width]), pairs(x12[:, width:])
+            if 2 in parts:
+                x3 = pairs(nt(rows_of(parity, j + 1), top))
             for i in range(step // 16):
-                y0 = nn(k_low, x0[i])
-                y12 = nn(k_mid, jnp.concatenate([x1[i], x2[i]], axis=0))
-                y3 = nn(k_top, x3[i])
-                for s, y in ((0, y0), (1, y12[: channels * 8]), (2, y12[channels * 8 :]), (3, y3)):
-                    z = y.reshape(channels, 8, 2 * width)
-                    at_row = s * width + row + 16 * i
-                    for w in range(channels):
-                        both = jnp.concatenate([z[w, :, :width], z[w, :, width:]], axis=0)
-                        lane = (w % 2) * width
-                        mixed[w // 2, at_row : at_row + 16, lane : lane + width] = both.astype(BF16)
-        wide = jnp.concatenate([low, mid[:width], mid[width:], top], axis=1)
+                if 0 in parts:
+                    put(0, i, nn(mix_low[prev], x0[i]))
+                if 1 in parts:
+                    y12 = nn(mix_mid[prev], jnp.concatenate([x1[i], x2[i]], axis=0))
+                    put(1, i, y12[: channels * 8])
+                    put(2, i, y12[channels * 8 :])
+                if 2 in parts:
+                    put(3, i, nn(mix_top[prev], x3[i]))
+        wide = {0: [low], 1: [mid[:width], mid[width:]], 2: [top]}
+        wide = jnp.concatenate([m for part in parts for m in wide[part]], axis=1)
+        start_row = {0: 0, 1: width, 2: 3 * width}[parts[0]]
         total = jnp.zeros((8, 2 * width), F32)
         for pair in range(channels // 2):
-            block = nn(wide, mixed[pair])
+            block = nn(wide, mixed[pair, start_row : start_row + wide.shape[1]])
+            if not first:
+                block = block + partial[prev, pair]
+            if not last:
+                partial[prev, pair] = block
+                continue
             r_all[turn, parity, j, 2 * pair] = block[:, :width].astype(BF16)
             r_all[turn, parity, j, 2 * pair + 1] = block[:, width:].astype(BF16)
             small = block * SMALL
             total = total + jnp.sum((small * small).reshape(width // 8, 8, 2 * width), axis=0)
             if pair > 0:
                 swap_pair(turn, j, pair - 1)
-        slot = (j >= 1).astype(jnp.int32)
-        squares[slot, turn] += total[:, :width] + total[:, width:]
-        swap_pair(turn, j, channels // 2 - 1)
+        if last:
+            slot = (j >= 1).astype(jnp.int32)
+            squares[slot, turn] += total[:, :width] + total[:, width:]
+            swap_pair(turn, j, channels // 2 - 1)
 
     def swap_wait(turn, j):
         part = r_all.at[turn, 1 - parity, j]
@@ -304,9 +332,9 @@
 
     @pl.when(role == 2)
     def _():
-        pl.semaphore_wait(barrier, 4)
-
-        @pl.loop(0, REACH)
+        pl.semaphore_wait(barrier, 6)
+
+        @pl.loop(0, REACH - 1)
         def _(k):
             for i in range(held):
                 for h in range(2):
@@ -314,12 +342,17 @@
                     def _():
                         ring_wait(k, i, h)
 
-                    @pl.when(k < REACH - 1)
+                    @pl.when(k < REACH - 2)
                     def _():
                         ring_copy(k, i, h).start()
 
+                    @pl.when(k == REACH - 2)
+                    def _():
+                        feed_far(i, h).start()
+
                     feed_half(k, i, h).start()
 
+        load_weights()
         edge_of(table_of(SITES - 1, mpo_ref, mask_ref, table), channels, coef)
         squares[...] = jnp.zeros_like(squares)
 
@@ -332,15 +365,17 @@
         pl.semaphore_wait(barrier, 2)
         for i in range(held):
             feed(3, 0, i, ring.at[0, i], feed_send.at[0, i]).start()
+        load_weights()
 
     @pl.when(works)
     def _():
         home = 2 - parity
-        pl.semaphore_wait(barrier, 5)
+        pl.semaphore_wait(barrier, 6)
         tell(0)
         feed(home, 0, 1 - parity, ring.at[0, 1 - parity], feed_send.at[0, 0]).start()
         pass_first(home).start()
         m_all[home, 0] = ring[0, parity]
+        load_weights()
         edge_of(table_of(SITES - 1, mpo_ref, mask_ref, table), channels, coef)
         squares[...] = jnp.zeros_like(squares)
         feed_wait(1 + parity, 0)
@@ -357,8 +392,7 @@
         told(1)
         tell(2)
 
-        @pl.loop(0, REACH)
-        def _(k):
+        def begin(k):
             feed_wait(0, k)
             start(m_all.at[0, k], r_all.at[0, parity, k], (k >= 1).astype(jnp.int32))
 
@@ -366,19 +400,47 @@
             def _():
                 swap(0, k).start()
 
-            @pl.loop(1, k + 1)
-            def _(t):
-                @pl.when(k == REACH - 1)
-                def _():
-                    feed_wait(t, k - t)
-
-                swap_wait(t - 1, k - t + parity)
-                advance(t, k - t)
+        @pl.loop(0, REACH)
+        def _(k):
+            @pl.when(k == REACH - 1)
+            def _():
+                @pl.loop(1, SITES)
+                def _(t):
+                    feed_wait(t, REACH - 1 - t)
+
+                    @pl.when(parity == 0)
+                    def _():
+                        swap_wait(t - 1, REACH - 1 - t)
+                        advance(t, REACH - 1 - t, (0, 1), last=False)
+
+                    @pl.when(parity == 1)
+                    def _():
+                        advance(t, REACH - 1 - t, (0,), last=False)
+
+            begin(k)
+
+            @pl.when(k < REACH - 1)
+            def _():
+                @pl.loop(1, k + 1)
+                def _(t):
+                    swap_wait(t - 1, k - t + parity)
+                    advance(t, k - t)
 
             @pl.when(k == 1)
             def _():
                 told(2)
                 tell(3)
+
+        @pl.loop(1, SITES)
+        def _(t):
+            @pl.when(parity == 0)
+            def _():
+                advance(t, REACH - 1 - t, (2,), first=False)
+
+            @pl.when(parity == 1)
+            def _():
+                swap_wait(t - 1, REACH - t)
+                advance(t, REACH - 1 - t, (1, 2), first=False)
 
         lane = ids(1, width, 1)
         row = jnp.zeros((1, width), F32)
@@ -394,6 +456,9 @@
                 @pl.when(jnp.logical_not(sum_self(kind, step)))
                 def _():
                     sum_copy(kind, step).start()
+
+            if kind == 0:
+                swap(SITES - 1, 0).start()
 
     def heard_all(count):
         part = heard.at[pl.ds(0, count)]
@@ -455,9 +520,9 @@
         for k in range(REACH):
             for i in range(held):
                 for h in range(2):
-                    if k < REACH - 1:
+                    if k < REACH - 2:
                         ring_copy(k, i, h).wait_send()
-                feed(0, k, i, ring.at[k, i], feed_send.at[k, i]).wait_send()
+                feed(0, k, i, ring.at[0, i], feed_send.at[k, i]).wait_send()
 
     @pl.when(role == 3)
     def _():
@@ -500,7 +565,7 @@
             pltpu.SMEM((1, held), jnp.int32),
             pltpu.SMEM((1, held, 3), jnp.int32),
             vmem((held, PHYS, width, width), BF16),
-            vmem((REACH, held, PHYS, width, width), BF16),
+            vmem((REACH - 1, held, PHYS, width, width), BF16),
             vmem((SITES, REACH, PHYS, width, width), BF16),
             vmem((SITES, 2, REACH, channels, width, width), BF16),
             vmem((SITES - 1, channels * 8, channels * 8), BF16),
@@ -509,6 +574,7 @@
             vmem((len(PAIRS), channels, 8, width), F32),
             vmem((channels * PHYS * PHYS, width), F32),
             vmem((channels // 2, PHYS * width, 2 * width), BF16),
+            vmem((SITES - 1, channels // 2, width, 2 * width), F32),
             vmem((2, SITES, 8, width), F32),
             vmem((1, width), F32),
             vmem((2 * places, 1, width), F32),

time: 50.4 us -> 55.4 us (1.099)
  Pallas kernels: 50.3 us -> 55.3 us
    pallas_call x1, Pallas kernels: 49.4 us -> 54.3 us  [on_device(): pl.pallas_call(kernel, out_shape=(jax.ShapeDtypeStruct(result, BF16), jax...]
where the time goes in v4:
time: 55.4 us; the launch traced here: 55.3 us
  Pallas kernels  55.3 us (100%)
    pallas_call x1, Pallas kernels, on_device(): pl.pallas_call(kernel, out_shape=(jax.ShapeDtypeStruct(result, BF16), jax...  54.3 us

profile of v4, /device:TPU:1, one launch (start us, length us, event | category | flops | bytes accessed | tf_op | source)
XLA Modules:
  0.0 55.3 jit_solution(15870542580759596743)
XLA Ops:
  0.0 54.3 %shard_map.55 = (bf16[2,10,128,128]{3,2,1,0:T(8,128)(2,1)S(1)}, f32[8,128]{1,0:T(8,128)S(1)}) custom-call(bf16[2,4,128,128]{3,2,1,0:T(8,128)(2,1)} %bitcast.4, bf16[4,10,4,4,10]{4,3,2,1,0:T(4,128)(2,1)} %bitcast.5, s32[10,4,10]{2,1,0:T(4,128)} %bitcast.6, s32[1,2]{1,0:T(1,128)} %size_in.1, s32[1,2,3]{2,1,0:T(2,128)} %live_in.1), custom_call_target="tpu_custom_call" | custom-call | tf_op jit(solution)/shard_map/pallas_call | solution.py:554
  54.4 0.9 %shard_map.56 = bf16[2,10,128,128]{3,2,1,0:T(8,128)(2,1)} custom-call(bf16[2,10,128,128]{3,2,1,0:T(8,128)(2,1)S(1)} %get-tuple-element.7.in_ref, f32[8,128]{1,0:T(8,128)S(1)} %get-tuple-element.8.scale_ref), custom_call_target="tpu_custom_call" | custom-call | tf_op jit(solution)/shard_map/pallas_call | solution.py:608

commit v5 on v3

--- a/solution.py
+++ b/solution.py
@@ -76,7 +76,7 @@
 
 def kernel(
     m_ref, mpo_in, mask_in, size_in, live_in, out_ref, scale_ref,
-    mpo_ref, mask_ref, size_ref, live_ref, raw, ring, m_all, r_all, mix_low, mix_mid, mix_top, coef, table, mixed, squares, mine, heard,
+    mpo_ref, mask_ref, size_ref, live_ref, raw, ring, m_all, r_all, mix_low, mix_mid, mix_top, coef, table, inner, mixed, squares, mine, heard,
     load_sem, ring_send, ring_recv, feed_send, feed_recv, pass_send, swap_send, swap_recv,
     sum_send, sum_recv, round_sem,
 ):
@@ -122,7 +122,7 @@
     def _():
         greet((hub, place), (hub + 1, place))
 
-    for load in loads:
+    for load in loads[:3]:
         load.wait()
     for i in range(held):
         sector = place * held + i
@@ -133,6 +133,10 @@
             block = jnp.where(ids(width, width, 0) < bound, raw[i, s].astype(F32), 0.0)
             ring[0, i, s] = block.astype(BF16)
 
+    def load_weights():
+        for load in loads[3:]:
+            load.wait()
+
     def remote(src, dst, send, recv, site_to, place_to):
         return pltpu.make_async_remote_copy(
             src_ref=src, dst_ref=dst, send_sem=send, recv_sem=recv,
@@ -188,7 +192,6 @@
         mid = blocks[1:3].reshape(2 * width, width)
         top = blocks[3]
         step = 32
-        total = jnp.zeros((8, width), F32)
         for row in range(0, width, step):
             g0 = nt(low[row : row + step], low)
             g1 = nt(mid[row : row + step], mid)
@@ -201,9 +204,11 @@
                 for i in range(1, len(PAIRS)):
                     block = block + parts[i] * coef[i, w][None]
                 target[w, row : row + step, :] = block.reshape(step, width).astype(BF16)
-                small = block * SMALL
-                total = total + jnp.sum(small * small, axis=0)
-        squares[slot, 0] += total
+
+        @pl.when(slot == 0)
+        def _():
+            small = target[...].astype(F32).reshape(channels * width // 8, 8, width) * SMALL
+            squares[0, 0] += jnp.sum(small * small, axis=0)
 
     def swap_part(turn, j, part):
         last = turn == SITES - 1
@@ -228,35 +233,42 @@
         top = m_all[turn, j, 3]
         step = 32
 
-        def pairs(x):
+        one = channels * 8
+
+        def keep(row, first, x):
             y = x.reshape(channels, step // 8, 8, width)
-            cut = lambda i: y[:, i].reshape(channels * 8, width)
-            return [
-                jnp.concatenate([cut(2 * j), cut(2 * j + 1)], axis=1).astype(BF16)
-                for j in range(step // 16)
-            ]
-
-        k_low, k_mid, k_top = mix_low[prev], mix_mid[prev], mix_top[prev]
+            for i in range(step // 16):
+                cut = [y[:, 2 * i + h].reshape(one, width) for h in range(2)]
+                both = jnp.concatenate(cut, axis=1).astype(BF16)
+                inner[row // 16 + i, first : first + one] = both
+
         for row in range(0, width, step):
             def rows_of(which, slot):
                 rows = r_all[prev, which, slot, :, row : row + step, :]
                 return rows.reshape(channels * step, width)
 
-            x0 = pairs(nt(rows_of(parity, j), low))
-            x12 = nt(rows_of(1 - parity, j + parity), mid)
-            x1, x2 = pairs(x12[:, :width]), pairs(x12[:, width:])
-            x3 = pairs(nt(rows_of(parity, j + 1), top))
-            for i in range(step // 16):
-                y0 = nn(k_low, x0[i])
-                y12 = nn(k_mid, jnp.concatenate([x1[i], x2[i]], axis=0))
-                y3 = nn(k_top, x3[i])
-                for s, y in ((0, y0), (1, y12[: channels * 8]), (2, y12[channels * 8 :]), (3, y3)):
-                    z = y.reshape(channels, 8, 2 * width)
-                    at_row = s * width + row + 16 * i
-                    for w in range(channels):
-                        both = jnp.concatenate([z[w, :, :width], z[w, :, width:]], axis=0)
-                        lane = (w % 2) * width
-                        mixed[w // 2, at_row : at_row + 16, lane : lane + width] = both.astype(BF16)
+            keep(row, 0, nt(rows_of(parity, j), low))
+            x = nt(rows_of(1 - parity, j + parity), mid)
+            keep(row, one, x[:, :width])
+            keep(row, 2 * one, x[:, width:])
+            keep(row, 3 * one, nt(rows_of(parity, j + 1), top))
+
+        def put(s, i, y):
+            z = y.reshape(channels, 8, 2 * width)
+            at_row = s * width + 16 * i
+            for w in range(channels):
+                both = jnp.concatenate([z[w, :, :width], z[w, :, width:]], axis=0)
+                lane = (w % 2) * width
+                mixed[w // 2, at_row : at_row + 16, lane : lane + width] = both.astype(BF16)
+
+        for i in range(width // 16):
+            put(0, i, nn(mix_low[prev], inner[i, :one]))
+        for i in range(width // 16):
+            y = nn(mix_mid[prev], inner[i, one : 3 * one])
+            put(1, i, y[:one])
+            put(2, i, y[one:])
+        for i in range(width // 16):
+            put(3, i, nn(mix_top[prev], inner[i, 3 * one :]))
         wide = jnp.concatenate([low, mid[:width], mid[width:], top], axis=1)
         total = jnp.zeros((8, 2 * width), F32)
         for pair in range(channels // 2):
@@ -320,6 +332,7 @@
 
                     feed_half(k, i, h).start()
 
+        load_weights()
         edge_of(table_of(SITES - 1, mpo_ref, mask_ref, table), channels, coef)
         squares[...] = jnp.zeros_like(squares)
 
@@ -332,6 +345,7 @@
         pl.semaphore_wait(barrier, 2)
         for i in range(held):
             feed(3, 0, i, ring.at[0, i], feed_send.at[0, i]).start()
+        load_weights()
 
     @pl.when(works)
     def _():
@@ -341,6 +355,7 @@
         feed(home, 0, 1 - parity, ring.at[0, 1 - parity], feed_send.at[0, 0]).start()
         pass_first(home).start()
         m_all[home, 0] = ring[0, parity]
+        load_weights()
         edge_of(table_of(SITES - 1, mpo_ref, mask_ref, table), channels, coef)
         squares[...] = jnp.zeros_like(squares)
         feed_wait(1 + parity, 0)
@@ -508,6 +523,7 @@
             vmem((SITES - 1, channels * 8, channels * 8), BF16),
             vmem((len(PAIRS), channels, 8, width), F32),
             vmem((channels * PHYS * PHYS, width), F32),
+            vmem((width // 16, PHYS * channels * 8, 2 * width), BF16),
             vmem((channels // 2, PHYS * width, 2 * width), BF16),
             vmem((2, SITES, 8, width), F32),
             vmem((1, width), F32),

time: 50.4 us -> 47.4 us (0.940)
  Pallas kernels: 50.3 us -> 47.3 us
    pallas_call x1, Pallas kernels: 49.4 us -> 46.4 us  [on_device(): pl.pallas_call(kernel, out_shape=(jax.ShapeDtypeStruct(result, BF16), jax...]
where the time goes in v5:
time: 47.4 us; the launch traced here: 47.3 us
  Pallas kernels  47.3 us (100%)
    pallas_call x1, Pallas kernels, on_device(): pl.pallas_call(kernel, out_shape=(jax.ShapeDtypeStruct(result, BF16), jax...  46.4 us

profile of v5, /device:TPU:1, one launch (start us, length us, event | category | flops | bytes accessed | tf_op | source)
XLA Modules:
  0.0 47.3 jit_solution(5605224838500183826)
XLA Ops:
  0.0 46.4 %shard_map.55 = (bf16[2,10,128,128]{3,2,1,0:T(8,128)(2,1)S(1)}, f32[8,128]{1,0:T(8,128)S(1)}) custom-call(bf16[2,4,128,128]{3,2,1,0:T(8,128)(2,1)} %bitcast.4, bf16[4,10,4,4,10]{4,3,2,1,0:T(4,128)(2,1)} %bitcast.5, s32[10,4,10]{2,1,0:T(4,128)} %bitcast.6, s32[1,2]{1,0:T(1,128)} %size_in.1, s32[1,2,3]{2,1,0:T(2,128)} %live_in.1), custom_call_target="tpu_custom_call" | custom-call | tf_op jit(solution)/shard_map/pallas_call | solution.py:504
  46.4 0.9 %shard_map.56 = bf16[2,10,128,128]{3,2,1,0:T(8,128)(2,1)} custom-call(bf16[2,10,128,128]{3,2,1,0:T(8,128)(2,1)S(1)} %get-tuple-element.7.in_ref, f32[8,128]{1,0:T(8,128)S(1)} %get-tuple-element.8.scale_ref), custom_call_target="tpu_custom_call" | custom-call | tf_op jit(solution)/shard_map/pallas_call | solution.py:558

commit v6 on v5

--- a/solution.py
+++ b/solution.py
@@ -277,11 +277,12 @@
             r_all[turn, parity, j, 2 * pair + 1] = block[:, width:].astype(BF16)
             small = block * SMALL
             total = total + jnp.sum((small * small).reshape(width // 8, 8, 2 * width), axis=0)
-            if pair > 0:
-                swap_pair(turn, j, pair - 1)
         slot = (j >= 1).astype(jnp.int32)
         squares[slot, turn] += total[:, :width] + total[:, width:]
-        swap_pair(turn, j, channels // 2 - 1)
+
+        @pl.when(swaps(turn, j))
+        def _():
+            swap(turn, j).start()
 
     def swap_wait(turn, j):
         part = r_all.at[turn, 1 - parity, j]
@@ -367,10 +368,6 @@
             mix_low[turn - 1] = spread(found, channels, 0, 1)
             mix_mid[turn - 1] = spread(found, channels, 1, 2)
             mix_top[turn - 1] = spread(found, channels, 3, 1)
-        feed_wait(1, 1)
-        pass_on(1, 1).start()
-        told(1)
-        tell(2)
 
         @pl.loop(0, REACH)
         def _(k):
@@ -389,6 +386,13 @@
 
                 swap_wait(t - 1, k - t + parity)
                 advance(t, k - t)
+
+            @pl.when(k == 0)
+            def _():
+                feed_wait(1, 1)
+                pass_on(1, 1).start()
+                told(1)
+                tell(2)
 
             @pl.when(k == 1)
             def _():

time: 47.4 us -> 44.6 us (0.941)
  Pallas kernels: 47.3 us -> 44.4 us
    pallas_call x1, Pallas kernels: 46.4 us -> 43.5 us  [on_device(): pl.pallas_call(kernel, out_shape=(jax.ShapeDtypeStruct(result, BF16), jax...]
where the time goes in v6:
time: 44.6 us; the launch traced here: 44.4 us
  Pallas kernels  44.4 us (100%)
    pallas_call x1, Pallas kernels, on_device(): pl.pallas_call(kernel, out_shape=(jax.ShapeDtypeStruct(result, BF16), jax...  43.5 us
    pallas_call x1, Pallas kernels, on_device(): pl.pallas_call(scaled, out_shape=jax.ShapeDtypeStruct(result, BF16), in_s...  0.92 us

profile of v6, /device:TPU:1, one launch (start us, length us, event | category | flops | bytes accessed | tf_op | source)
XLA Modules:
  0.0 44.4 jit_solution(6415840071197350656)
XLA Ops:
  0.0 43.5 %shard_map.55 = (bf16[2,10,128,128]{3,2,1,0:T(8,128)(2,1)S(1)}, f32[8,128]{1,0:T(8,128)S(1)}) custom-call(bf16[2,4,128,128]{3,2,1,0:T(8,128)(2,1)} %bitcast.4, bf16[4,10,4,4,10]{4,3,2,1,0:T(4,128)(2,1)} %bitcast.5, s32[10,4,10]{2,1,0:T(4,128)} %bitcast.6, s32[1,2]{1,0:T(1,128)} %size_in.1, s32[1,2,3]{2,1,0:T(2,128)} %live_in.1), custom_call_target="tpu_custom_call" | custom-call | tf_op jit(solution)/shard_map/pallas_call | solution.py:508
  43.5 0.9 %shard_map.56 = bf16[2,10,128,128]{3,2,1,0:T(8,128)(2,1)} custom-call(bf16[2,10,128,128]{3,2,1,0:T(8,128)(2,1)S(1)} %get-tuple-element.7.in_ref, f32[8,128]{1,0:T(8,128)S(1)} %get-tuple-element.8.scale_ref), custom_call_target="tpu_custom_call" | custom-call | tf_op jit(solution)/shard_map/pallas_call | solution.py:562

commit v7 on v6

--- a/solution.py
+++ b/solution.py
@@ -414,43 +414,6 @@
                 def _():
                     sum_copy(kind, step).start()
 
-    def heard_all(count):
-        part = heard.at[pl.ds(0, count)]
-        remote(part, part, sum_send.at[0, 0], sum_recv, site, at(1)).wait_recv()
-
-    @pl.when(role == 3)
-    def _():
-        for i in range(held):
-            part = r_all.at[3, i, 0]
-            remote(
-                part, part, swap_send.at[3, 0], swap_recv.at[3, i], hub + i, place
-            ).wait_recv()
-
-    @pl.when(role == 1)
-    def _():
-        swap_wait(1, 0)
-
-    @pl.when(works)
-    def _():
-        heard_all(2 * places - 1)
-
-    @pl.when(role >= 2)
-    def _():
-        heard_all(2 * places)
-
-    turn = jnp.where(role == 3, 3, 2 - role)
-    sums = jnp.sum(heard[...].reshape(2 * places, width), axis=0, keepdims=True)
-    entries = float(places * held * channels * width * width)
-    unit = jnp.ones((1, 1), F32)
-    chosen = unit
-    for t in range(SITES):
-        square = sums[:, t : t + 1] * (1.0 / (SMALL * SMALL * entries)) * unit * unit
-        unit = unit * lax.rsqrt(square + EPSILON)
-        chosen = jnp.where(turn == t, unit, chosen)
-    scale_ref[...] = jnp.broadcast_to(chosen, scale_ref.shape)
-    for i in range(held):
-        out_ref[i] = r_all[turn, i, 0]
-
     @pl.when(works)
     def _():
         home = 2 - parity
@@ -482,6 +445,44 @@
     def _():
         for i in range(held):
             feed(3, 0, i, ring.at[0, i], feed_send.at[0, i]).wait_send()
+
+    def heard_all(count):
+        part = heard.at[pl.ds(0, count)]
+        remote(part, part, sum_send.at[0, 0], sum_recv, site, at(1)).wait_recv()
+
+    @pl.when(role == 3)
+    def _():
+        for i in range(held):
+            part = r_all.at[3, i, 0]
+            remote(
+                part, part, swap_send.at[3, 0], swap_recv.at[3, i], hub + i, place
+            ).wait_recv()
+
+    @pl.when(role == 1)
+    def _():
+        swap_wait(1, 0)
+
+    turn = jnp.where(role == 3, 3, 2 - role)
+    for i in range(held):
+        out_ref[i] = r_all[turn, i, 0]
+
+    @pl.when(works)
+    def _():
+        heard_all(2 * places - 1)
+
+    @pl.when(role >= 2)
+    def _():
+        heard_all(2 * places)
+
+    sums = jnp.sum(heard[...].reshape(2 * places, width), axis=0, keepdims=True)
+    entries = float(places * held * channels * width * width)
+    unit = jnp.ones((1, 1), F32)
+    chosen = unit
+    for t in range(SITES):
+        square = sums[:, t : t + 1] * (1.0 / (SMALL * SMALL * entries)) * unit * unit
+        unit = unit * lax.rsqrt(square + EPSILON)
+        chosen = jnp.where(turn == t, unit, chosen)
+    scale_ref[...] = jnp.broadcast_to(chosen, scale_ref.shape)
 
 
 def scaled(in_ref, scale_ref, out_ref, final, done_sem):

time: 44.6 us -> 44.2 us (level)
  no operation moved by 1% of the time
where the time goes in v7:
time: 44.2 us; the launch traced here: 44.1 us
  Pallas kernels  44.1 us (100%)
    pallas_call x1, Pallas kernels, on_device(): pl.pallas_call(kernel, out_shape=(jax.ShapeDtypeStruct(result, BF16), jax...  43.1 us
    pallas_call x1, Pallas kernels, on_device(): pl.pallas_call(scaled, out_shape=jax.ShapeDtypeStruct(result, BF16), in_s...  0.92 us

profile of v7, /device:TPU:1, one launch (start us, length us, event | category | flops | bytes accessed | tf_op | source)
XLA Modules:
  0.0 44.1 jit_solution(5883575938832556566)
XLA Ops:
  0.0 43.1 %shard_map.55 = (bf16[2,10,128,128]{3,2,1,0:T(8,128)(2,1)S(1)}, f32[8,128]{1,0:T(8,128)S(1)}) custom-call(bf16[2,4,128,128]{3,2,1,0:T(8,128)(2,1)} %bitcast.4, bf16[4,10,4,4,10]{4,3,2,1,0:T(4,128)(2,1)} %bitcast.5, s32[10,4,10]{2,1,0:T(4,128)} %bitcast.6, s32[1,2]{1,0:T(1,128)} %size_in.1, s32[1,2,3]{2,1,0:T(2,128)} %live_in.1), custom_call_target="tpu_custom_call" | custom-call | tf_op jit(solution)/shard_map/pallas_call | solution.py:509
  43.2 0.9 %shard_map.56 = bf16[2,10,128,128]{3,2,1,0:T(8,128)(2,1)} custom-call(bf16[2,10,128,128]{3,2,1,0:T(8,128)(2,1)S(1)} %get-tuple-element.7.in_ref, f32[8,128]{1,0:T(8,128)S(1)} %get-tuple-element.8.scale_ref), custom_call_target="tpu_custom_call" | custom-call | tf_op jit(solution)/shard_map/pallas_call | solution.py:563

commit v8 on v7

--- a/solution.py
+++ b/solution.py
@@ -277,12 +277,13 @@
             r_all[turn, parity, j, 2 * pair + 1] = block[:, width:].astype(BF16)
             small = block * SMALL
             total = total + jnp.sum((small * small).reshape(width // 8, 8, 2 * width), axis=0)
-        slot = (j >= 1).astype(jnp.int32)
-        squares[slot, turn] += total[:, :width] + total[:, width:]
 
         @pl.when(swaps(turn, j))
         def _():
             swap(turn, j).start()
+
+        slot = (j >= 1).astype(jnp.int32)
+        squares[slot, turn] += total[:, :width] + total[:, width:]
 
     def swap_wait(turn, j):
         part = r_all.at[turn, 1 - parity, j]
@@ -407,7 +408,11 @@
         heard[parity * places + place] = row
         told(3)
 
-        for kind in range(4):
+        @pl.loop(0, places)
+        def _(step):
+            sum_copy(0, step).start()
+
+        for kind in range(1, 4):
             @pl.loop(0, places)
             def _(step):
                 @pl.when(jnp.logical_not(sum_self(kind, step)))

time: 44.2 us -> 44.2 us (level)
  no operation moved by 1% of the time
where the time goes in v8:
time: 44.2 us; the launch traced here: 44.1 us
  Pallas kernels  44.1 us (100%)
    pallas_call x1, Pallas kernels, on_device(): pl.pallas_call(kernel, out_shape=(jax.ShapeDtypeStruct(result, BF16), jax...  43.1 us
    pallas_call x1, Pallas kernels, on_device(): pl.pallas_call(scaled, out_shape=jax.ShapeDtypeStruct(result, BF16), in_s...  0.92 us

profile of v8, /device:TPU:1, one launch (start us, length us, event | category | flops | bytes accessed | tf_op | source)
XLA Modules:
  0.0 44.1 jit_solution(5051610537987857702)
XLA Ops:
  0.0 43.1 %shard_map.55 = (bf16[2,10,128,128]{3,2,1,0:T(8,128)(2,1)S(1)}, f32[8,128]{1,0:T(8,128)S(1)}) custom-call(bf16[2,4,128,128]{3,2,1,0:T(8,128)(2,1)} %bitcast.4, bf16[4,10,4,4,10]{4,3,2,1,0:T(4,128)(2,1)} %bitcast.5, s32[10,4,10]{2,1,0:T(4,128)} %bitcast.6, s32[1,2]{1,0:T(1,128)} %size_in.1, s32[1,2,3]{2,1,0:T(2,128)} %live_in.1), custom_call_target="tpu_custom_call" | custom-call | tf_op jit(solution)/shard_map/pallas_call | solution.py:514
  43.1 0.9 %shard_map.56 = bf16[2,10,128,128]{3,2,1,0:T(8,128)(2,1)} custom-call(bf16[2,10,128,128]{3,2,1,0:T(8,128)(2,1)S(1)} %get-tuple-element.7.in_ref, f32[8,128]{1,0:T(8,128)S(1)} %get-tuple-element.8.scale_ref), custom_call_target="tpu_custom_call" | custom-call | tf_op jit(solution)/shard_map/pallas_call | solution.py:568
